TPU v7x, 32 devices: a whole 2x2x4 slice. The times are simulated.
32 devices in a mesh: fsdp: 4 (over x, core), ctx: 2 (over y), tp: 4 (over z).
Axes of the slice: x: 2, y: 2, z: 4, core: 2. Of those that a mesh axis runs over, the one named last changes fastest.
Arguments:
- inputs: bfloat16 [2048, 8, 768], P('ctx', 'fsdp'), may hold values from -6 to 6
- thoughts: bfloat16 [6, 8, 768], P(None, 'fsdp'), may hold values from -6 to 6
- positions: int32 [6, 8], P(None, 'fsdp'), may hold values from 0 to 2047, as said below
- lengths: int32 [8, 3], P('fsdp'), may hold values from 1 to 1024, 2048 in all within a row
- w_qkv: bfloat16 [3, 768, 768], P(None, 'fsdp', 'tp'), may hold values from -0.21875 to 0.21875
- w_out: bfloat16 [768, 768], P('tp', 'fsdp'), may hold values from -3.5 to 3.5
- w_fc: bfloat16 [768, 3072], P('fsdp', 'tp'), may hold values from -0.21875 to 0.21875
- w_proj: bfloat16 [3072, 768], P('tp', 'fsdp'), may hold values from -0.109375 to 0.109375
- norm_gains: bfloat16 [2, 768], P(None, 'fsdp'), may hold values from 0.099609375 to 1.8984375
- norm_biases: bfloat16 [2, 768], P(None, 'fsdp'), may hold values from -0.14941406 to 0.14941406
- out_grad: bfloat16 [2048, 8, 768], P('ctx', 'fsdp'), may hold values from -6 to 6
Outputs:
- output: bfloat16 [2048, 8, 768], P('ctx', 'fsdp')
- d_inputs: float32 [2048, 8, 768], P('ctx', 'fsdp')
- d_thoughts: float32 [6, 8, 768], P(None, 'fsdp')
- d_w_qkv: float32 [3, 768, 768], P(None, 'fsdp', 'tp')
- d_w_out: float32 [768, 768], P('tp', 'fsdp')
- d_w_fc: float32 [768, 3072], P('fsdp', 'tp')
- d_w_proj: float32 [3072, 768], P('tp', 'fsdp')
- d_norm_gains: float32 [2, 768], P(None, 'fsdp')
- d_bias_first: float32 [768], P('fsdp')
- d_bias_second: float32 [768], P('fsdp')
Inputs may be any that keep to these rules, and one draw needn't show every extreme that they name: Each entry is a position of its sequence; the 6 positions of one sequence are distinct.
All inputs are finite; a program needn't handle non-finite values.
Results may differ from a plain program's by a relative error of at most 0.017.
Values may be sent and summed in bfloat16 or wider, within the bound.
A program may use at most 192 MiB of HBM per device.

v0:
```python
import jax
import jax.numpy as jnp
from jax import lax
from jax.sharding import PartitionSpec as P

HEAD_DIM = 64


EPSILON = 1e-05
NEGATIVE = -1000000000.0
PRECISE = lax.Precision.HIGHEST


def norm_rows(values, gain_row, offset):
    centre = jnp.mean(values, axis=-1, keepdims=True)
    shifted = values - centre
    spread = jnp.mean(shifted * shifted, axis=-1, keepdims=True)
    return shifted * lax.rsqrt(spread + EPSILON) * gain_row + offset


def gelu_tanh(values):
    return jax.nn.gelu(values, approximate=True)


def segment_ids(lengths, length):
    doc_ends = jnp.cumsum(lengths, axis=1, dtype=jnp.int32)
    places = jnp.arange(length, dtype=jnp.int32)
    return jnp.sum((places[:, None, None] >= doc_ends[None, :, :]).astype(jnp.int32), axis=2)


def seq_group(source, block_index, group_size):
    return lax.dynamic_slice_in_dim(source, block_index * group_size, group_size, 1)


def ungroup(stacked, row_count, seq_count):
    return jnp.moveaxis(stacked, 0, 1).reshape(row_count, seq_count, -1)


def heads_first(values):
    return jnp.moveaxis(values, 2, 0)


def heads_back(values):
    return jnp.moveaxis(values, 0, 2)


def score_head(query_head, key_head, query_pos, key_pos, query_seg, key_seg, score_scale):
    scores = (
        jnp.einsum("qgd,kgd->gqk", query_head, key_head, preferred_element_type=jnp.float32)
        * score_scale
    )
    causal = query_pos[:, None] >= key_pos[None, :]
    same_doc = query_seg.T[:, :, None] == key_seg.T[:, None, :]
    allowed = causal[None] & same_doc
    return (jnp.where(allowed, scores, NEGATIVE), allowed)


def head_back(
    query_head,
    key_head,
    value_head,
    grad_head,
    log_head,
    query_pos,
    key_pos,
    query_seg,
    key_seg,
    score_scale,
):
    scores, allowed = score_head(
        query_head, key_head, query_pos, key_pos, query_seg, key_seg, score_scale
    )
    attn_probs = jnp.where(allowed, jnp.exp(scores - log_head[..., None]), 0.0)
    d_probs = jnp.einsum("qgd,kgd->gqk", grad_head, value_head, preferred_element_type=jnp.float32)
    row_delta = jnp.sum(attn_probs * d_probs, axis=-1)
    d_scores = (attn_probs * (d_probs - row_delta[..., None])).astype(jnp.bfloat16)
    d_query = (
        jnp.einsum("gqk,kgd->qgd", d_scores, key_head, preferred_element_type=jnp.float32)
        * score_scale
    )
    d_keys = (
        jnp.einsum("gqk,qgd->kgd", d_scores, query_head, preferred_element_type=jnp.float32)
        * score_scale
    )
    d_values = jnp.einsum(
        "gqk,qgd->kgd",
        attn_probs.astype(jnp.bfloat16),
        grad_head,
        preferred_element_type=jnp.float32,
    )
    return (d_query, row_delta, d_keys, d_values)


def local(
    inputs,
    thoughts,
    positions,
    lengths,
    w_qkv,
    w_out,
    w_fc,
    w_proj,
    norm_gains,
    norm_biases,
    out_grad,
):
    row_count, seq_count, model_width = inputs.shape
    ctx_count = lax.axis_size("ctx")
    seq_length = row_count * ctx_count
    first_row = lax.axis_index("ctx") * row_count
    group_size = max(1, min(seq_count, 512 // row_count))
    block_count = seq_count // group_size
    token_count = row_count * seq_count
    score_scale = HEAD_DIM ** (-0.5)
    qkv_full, out_full, fc_full, proj_full, gain_rows, offset_rows = (
        lax.all_gather(w_qkv, "fsdp", axis=1, tiled=True),
        lax.all_gather(w_out, "fsdp", axis=1, tiled=True),
        lax.all_gather(w_fc, "fsdp", axis=0, tiled=True),
        lax.all_gather(w_proj, "fsdp", axis=1, tiled=True),
        lax.all_gather(norm_gains, "fsdp", axis=1, tiled=True),
        lax.all_gather(norm_biases, "fsdp", axis=1, tiled=True),
    )
    gain_rows = gain_rows.astype(jnp.float32)
    offset_rows = offset_rows.astype(jnp.float32)
    local_width = qkv_full.shape[2]
    local_heads = local_width // HEAD_DIM
    qkv_matrix = jnp.transpose(qkv_full, (1, 0, 2)).reshape(model_width, 3 * local_width)
    row_places = first_row + jnp.arange(row_count, dtype=jnp.int32)
    key_places = jnp.arange(seq_length, dtype=jnp.int32)
    select = (row_places[:, None, None] == positions[None, :, :]).astype(jnp.float32)
    keep_rows = 1.0 - jnp.sum(select, axis=1)
    start_rows = inputs.astype(jnp.float32) * keep_rows[:, :, None] + jnp.einsum(
        "rts,tsd->rsd", select, thoughts.astype(jnp.float32), precision=PRECISE
    )
    start_flat = start_rows.reshape(token_count, model_width)
    normed = norm_rows(start_flat, gain_rows[0], offset_rows[0]).astype(jnp.bfloat16)
    projected = jnp.dot(normed, qkv_matrix, preferred_element_type=jnp.float32)
    queries = (
        projected[:, :local_width]
        .astype(jnp.bfloat16)
        .reshape(row_count, seq_count, local_heads, HEAD_DIM)
    )
    keys_values = (
        projected[:, local_width:]
        .astype(jnp.bfloat16)
        .reshape(row_count, seq_count, 2 * local_width)
    )
    seg_all = segment_ids(lengths, seq_length)
    seg_rows = lax.dynamic_slice_in_dim(seg_all, first_row, row_count, 0)

    def split_pairs(whole_kv, count):
        key_part = whole_kv[..., :local_width].reshape(count, group_size, local_heads, HEAD_DIM)
        value_part = whole_kv[..., local_width:].reshape(count, group_size, local_heads, HEAD_DIM)
        return (key_part, value_part)

    def forward_block(block_index):
        whole_kv = lax.all_gather(
            seq_group(keys_values, block_index, group_size), "ctx", axis=0, tiled=True
        )
        key_part, value_part = split_pairs(whole_kv, seq_length)
        query_seg = seq_group(seg_rows, block_index, group_size)
        key_seg = seq_group(seg_all, block_index, group_size)

        def forward_one_head(triple):
            query_head, key_head, value_head = triple
            scores, allowed = score_head(
                query_head, key_head, row_places, key_places, query_seg, key_seg, score_scale
            )
            top_score = jnp.max(scores, axis=-1, keepdims=True)
            raised = jnp.exp(scores - top_score)
            row_total = jnp.sum(raised, axis=-1, keepdims=True)
            attn_probs = (raised / row_total).astype(jnp.bfloat16)
            mixed_rows = jnp.einsum(
                "gqk,kgd->qgd", attn_probs, value_head, preferred_element_type=jnp.float32
            )
            return (mixed_rows, (top_score + jnp.log(row_total))[..., 0])

        mixed_heads, log_heads = lax.map(
            forward_one_head,
            (
                heads_first(seq_group(queries, block_index, group_size)),
                heads_first(key_part),
                heads_first(value_part),
            ),
        )
        return (heads_back(mixed_heads), jnp.moveaxis(log_heads, 0, 1))

    attended, log_totals = lax.map(forward_block, jnp.arange(block_count))
    attended_b = (
        ungroup(attended, row_count, seq_count)
        .reshape(token_count, local_width)
        .astype(jnp.bfloat16)
    )
    attention = lax.psum(jnp.dot(attended_b, out_full, preferred_element_type=jnp.float32), "tp")
    middle = start_flat + attention
    normed_mid = norm_rows(middle, gain_rows[1], offset_rows[1]).astype(jnp.bfloat16)
    expanded = jnp.dot(normed_mid, fc_full, preferred_element_type=jnp.float32)
    activated = gelu_tanh(expanded).astype(jnp.bfloat16)
    feedforward = lax.psum(
        jnp.dot(activated, proj_full, preferred_element_type=jnp.float32).astype(jnp.bfloat16), "tp"
    ).astype(jnp.float32)
    output = (middle + feedforward).astype(jnp.bfloat16).reshape(row_count, seq_count, model_width)
    grad_rows = out_grad.reshape(token_count, model_width)
    d_proj = jnp.einsum("nf,nd->fd", activated, grad_rows, preferred_element_type=jnp.float32)
    d_activated = jnp.einsum("nd,fd->nf", grad_rows, proj_full, preferred_element_type=jnp.float32)
    gelu_back = jax.vjp(gelu_tanh, expanded)[1]
    d_expanded = gelu_back(d_activated)[0].astype(jnp.bfloat16)
    d_fc = jnp.einsum("nd,nf->df", normed_mid, d_expanded, preferred_element_type=jnp.float32)
    d_normed_mid = lax.psum(
        jnp.einsum("nf,df->nd", d_expanded, fc_full, preferred_element_type=jnp.float32), "tp"
    )
    mid_back = jax.vjp(norm_rows, middle, gain_rows[1], offset_rows[1])[1]
    d_middle, d_gain_mid, d_offset_mid = mid_back(d_normed_mid)
    d_middle = d_middle + grad_rows.astype(jnp.float32)
    d_attention = d_middle.astype(jnp.bfloat16)
    d_out = jnp.einsum("nc,nd->cd", attended_b, d_attention, preferred_element_type=jnp.float32)
    d_attended = jnp.einsum("nd,cd->nc", d_attention, out_full, preferred_element_type=jnp.float32)
    d_attended = d_attended.astype(jnp.bfloat16).reshape(
        row_count, seq_count, local_heads, HEAD_DIM
    )

    def fetch_keys(block_index):
        whole_kv = lax.all_gather(
            seq_group(keys_values, block_index, group_size), "ctx", axis=0, tiled=True
        )
        return split_pairs(whole_kv, seq_length)

    def query_side(block_index, log_block):
        key_part, value_part = fetch_keys(block_index)
        query_seg = seq_group(seg_rows, block_index, group_size)
        key_seg = seq_group(seg_all, block_index, group_size)

        def query_one_head(five):
            query_head, key_head, value_head, grad_head, log_head = five
            return head_back(
                query_head,
                key_head,
                value_head,
                grad_head,
                log_head,
                row_places,
                key_places,
                query_seg,
                key_seg,
                score_scale,
            )

        return lax.map(
            query_one_head,
            (
                heads_first(seq_group(queries, block_index, group_size)),
                heads_first(key_part),
                heads_first(value_part),
                heads_first(seq_group(d_attended, block_index, group_size)),
                jnp.moveaxis(log_block, 1, 0),
            ),
        )

    def backward_block(block_pair):
        block_index, log_block = block_pair
        d_query, row_delta, d_keys, d_values = query_side(block_index, log_block)
        term = jnp.concatenate(
            [
                heads_back(d_keys).reshape(seq_length, group_size, local_width),
                heads_back(d_values).reshape(seq_length, group_size, local_width),
            ],
            axis=-1,
        )
        return (
            heads_back(d_query),
            lax.psum_scatter(
                term.astype(jnp.bfloat16), "ctx", scatter_dimension=0, tiled=True
            ).astype(jnp.float32),
        )

    d_queries, d_kv = lax.map(backward_block, (jnp.arange(block_count), log_totals))
    d_query_rows = ungroup(d_queries, row_count, seq_count).reshape(token_count, local_width)
    d_kv_rows = ungroup(d_kv, row_count, seq_count).reshape(token_count, 2 * local_width)
    d_projected = jnp.concatenate([d_query_rows, d_kv_rows], axis=1).astype(jnp.bfloat16)
    d_qkv = jnp.einsum("nd,nc->dc", normed, d_projected, preferred_element_type=jnp.float32)
    d_qkv = jnp.transpose(d_qkv.reshape(model_width, 3, local_width), (1, 0, 2))
    d_normed = lax.psum(
        jnp.einsum("nc,dc->nd", d_projected, qkv_matrix, preferred_element_type=jnp.float32).astype(
            jnp.bfloat16
        ),
        "tp",
    ).astype(jnp.float32)
    first_back = jax.vjp(norm_rows, start_flat, gain_rows[0], offset_rows[0])[1]
    d_start, d_gain_first, d_offset_first = first_back(d_normed)
    d_start_rows = (d_start + d_middle).reshape(row_count, seq_count, model_width)
    d_inputs = d_start_rows * keep_rows[:, :, None]
    d_thoughts = jnp.einsum("rts,rsd->tsd", select, d_start_rows, precision=PRECISE)
    d_gains = jnp.stack([d_gain_first, d_gain_mid])
    d_offsets = jnp.stack([d_offset_first, d_offset_mid])
    shares = (
        lax.psum_scatter(
            d_qkv.astype(jnp.bfloat16), "fsdp", scatter_dimension=1, tiled=True
        ).astype(jnp.float32),
        lax.psum_scatter(
            d_out.astype(jnp.bfloat16), "fsdp", scatter_dimension=1, tiled=True
        ).astype(jnp.float32),
        lax.psum_scatter(d_fc.astype(jnp.bfloat16), "fsdp", scatter_dimension=0, tiled=True).astype(
            jnp.float32
        ),
        lax.psum_scatter(
            d_proj.astype(jnp.bfloat16), "fsdp", scatter_dimension=1, tiled=True
        ).astype(jnp.float32),
        lax.psum_scatter(
            d_gains.astype(jnp.bfloat16), "fsdp", scatter_dimension=1, tiled=True
        ).astype(jnp.float32),
        lax.psum_scatter(
            d_offsets.astype(jnp.bfloat16), "fsdp", scatter_dimension=1, tiled=True
        ).astype(jnp.float32),
    )
    summed = (
        lax.psum(shares[0].astype(jnp.bfloat16), "ctx").astype(jnp.float32),
        lax.psum(shares[1].astype(jnp.bfloat16), "ctx").astype(jnp.float32),
        lax.psum(shares[2].astype(jnp.bfloat16), "ctx").astype(jnp.float32),
        lax.psum(shares[3].astype(jnp.bfloat16), "ctx").astype(jnp.float32),
        lax.psum(shares[4].astype(jnp.bfloat16), "ctx").astype(jnp.float32),
        lax.psum(shares[5].astype(jnp.bfloat16), "ctx").astype(jnp.float32),
        lax.psum(d_thoughts.astype(jnp.bfloat16), "ctx").astype(jnp.float32),
    )
    return (
        output,
        d_inputs,
        summed[6],
        summed[0],
        summed[1],
        summed[2],
        summed[3],
        summed[4],
        summed[5][0],
        summed[5][1],
    )


def solution(mesh):
    in_specs = (
        P("ctx", "fsdp", None),
        P(None, "fsdp", None),
        P(None, "fsdp"),
        P("fsdp", None),
        P(None, "fsdp", "tp"),
        P("tp", "fsdp"),
        P("fsdp", "tp"),
        P("tp", "fsdp"),
        P(None, "fsdp"),
        P(None, "fsdp"),
        P("ctx", "fsdp", None),
    )
    out_specs = (
        P("ctx", "fsdp", None),
        P("ctx", "fsdp", None),
        P(None, "fsdp", None),
        P(None, "fsdp", "tp"),
        P("tp", "fsdp"),
        P("fsdp", "tp"),
        P("tp", "fsdp"),
        P(None, "fsdp"),
        P("fsdp"),
        P("fsdp"),
    )
    return jax.shard_map(local, mesh=mesh, in_specs=in_specs, out_specs=out_specs, check_vma=False)
```

profile of v0, /device:TPU:25, one launch (start us, length us, event | category | flops | bytes accessed | tf_op | source)
XLA Modules:
  0.0 1462.6 jit_solution(1052572031871166158)
XLA Ops:
  22.5 13.0 all_gather.26
  70.7 122.6 %while.55 = (s32[]{:T(128)}, bf16[2,1024,1,3,64]{1,4,3,2,0:T(8,128)(2,1)}, f32[2,1,3,1024]{3,0,2,1:T(2,128)S(1)}, s32[2]{0:T(128)S(1)}, bf16[1024,2,3,64]{0,3,1,...) while((s32[]{:T(128)}, ...), condition=%wide.region_10.11_spmd.clone, body=%wide.region_5.10_spmd.clone.sunk | while | flops 559939584 | bytes 42727944 | solution.py:188
  75.5 27.0 %all-gather.11.cloned.1.call-done = bf16[2048,1,384]{0,2,1:T(8,128)(2,1)} async-done(((bf16[1024,1,384]{0,2,1:T(8,128)(2,1)}), bf16[2048,1,384]{0,2,1:T(8,128)(2,1)}) %all-gather.11.cloned.1.call-update) | async-done | bytes 1572880 | tf_op jit(solution)/shard_map/while/body/eval_jaxpr/all_gather | solution.py:157
  105.0 25.7 %while.58 = (s32[]{:T(128)}, bf16[3,1024,1,64]{1,3,2,0:T(8,128)(2,1)}, f32[3,1,1024]{2,1,0:T(1,128)S(1)}, bf16[3,2048,1,64]{1,3,2,0:T(8,128)(2,1)}, s32[1024]{0:...) while((s32[]{:T(128)}, ...), condition=%wide.region_9.9_spmd, body=%wide.region_6.8_spmd.sunk | while | flops 559938560 | bytes 29296816 | solution.py:178
  136.9 26.5 %all-gather.11.cloned.1.call-done = bf16[2048,1,384]{0,2,1:T(8,128)(2,1)} async-done(((bf16[1024,1,384]{0,2,1:T(8,128)(2,1)}), bf16[2048,1,384]{0,2,1:T(8,128)(2,1)}) %all-gather.11.cloned.1.call-update) | async-done | bytes 1572880 | tf_op jit(solution)/shard_map/while/body/eval_jaxpr/all_gather | solution.py:157
  165.8 25.7 %while.58 = (s32[]{:T(128)}, bf16[3,1024,1,64]{1,3,2,0:T(8,128)(2,1)}, f32[3,1,1024]{2,1,0:T(1,128)S(1)}, bf16[3,2048,1,64]{1,3,2,0:T(8,128)(2,1)}, s32[1024]{0:...) while((s32[]{:T(128)}, ...), condition=%wide.region_9.9_spmd, body=%wide.region_6.8_spmd.sunk | while | flops 559938560 | bytes 29296816 | solution.py:178
  202.2 9.3 all_gather.27
  216.6 10.3 copy.142
  226.9 7.7 reshape.379
  234.6 8.5 reshape.374
  243.1 7.4 fusion.95
  250.5 185.9 %all-reduce.8.cloned.1.call-done = f32[2048,768]{1,0:T(8,128)} async-done(((f32[2048,768]{1,0:T(8,128)}), f32[2048,768]{1,0:T(8,128)}) %all-reduce.8.cloned.1.call-update) | async-done | bytes 6291472 | tf_op jit(solution)/shard_map/psum | solution.py:194
  446.7 10.1 fusion.62
  463.0 7.8 reshape.398
  470.8 214.2 %all-reduce.10.cloned.1.call-done = f32[2048,768]{1,0:T(8,128)} async-done(((f32[2048,768]{1,0:T(8,128)}), f32[2048,768]{1,0:T(8,128)}) %all-reduce.10.cloned.1.call-update) | async-done | bytes 6291472 | tf_op jit(solution)/shard_map/psum | solution.py:209
  712.3 282.4 %while.57 = (s32[]{:T(128)}, bf16[2,1024,1,3,64]{1,4,3,2,0:T(8,128)(2,1)}, bf16[2,1024,1,384]{1,3,2,0:T(8,128)(2,1)}, s32[2]{0:T(128)S(1)}, bf16[1024,2,3,64]{0,...) while((s32[]{:T(128)}, ...), condition=%wide.region_23.24_spmd.clone, body=%wide.region_18.23_spmd.clone.sunk | while | flops 1373175808 | bytes 154253136 | solution.py:276
  717.7 27.2 %all-gather.13.cloned.1.call-done = bf16[2048,1,384]{0,2,1:T(8,128)(2,1)} async-done(((bf16[1024,1,384]{0,2,1:T(8,128)(2,1)}), bf16[2048,1,384]{0,2,1:T(8,128)(2,1)}) %all-gather.13.cloned.1.call-update) | async-done | bytes 1572880 | tf_op jit(solution)/shard_map/while/body/eval_jaxpr/all_gather | solution.py:223
  747.6 75.5 %while.59 = (s32[]{:T(128)}, bf16[3,1024,1,64]{1,3,2,0:T(8,128)(2,1)}, bf16[3,2048,1,64]{1,3,2,0:T(8,128)(2,1)}, bf16[3,2048,1,64]{1,3,2,0:T(8,128)(2,1)}, bf16[...) while((s32[]{:T(128)}, ...), condition=%wide.region_21.21_spmd, body=%wide.region_19.20_spmd.sunk | while | flops 1369635840 | bytes 108578080 | solution.py:248
  827.7 24.5 %reduce-scatter.28.cloned.1.call-done = bf16[1024,1,384]{0,2,1:T(8,128)(2,1)} async-done(((bf16[2048,1,384]{0,2,1:T(8,128)(2,1)}), bf16[1024,1,384]{0,2,1:T(8,128)(2,1)}) %reduce-scatter.28.cloned.1.call-update) | async-done | bytes 786448 | tf_op jit(solution)/shard_map/while/body/eval_jaxpr/reduce_scatter | solution.py:271
  859.2 26.1 %all-gather.13.cloned.1.call-done = bf16[2048,1,384]{0,2,1:T(8,128)(2,1)} async-done(((bf16[1024,1,384]{0,2,1:T(8,128)(2,1)}), bf16[2048,1,384]{0,2,1:T(8,128)(2,1)}) %all-gather.13.cloned.1.call-update) | async-done | bytes 1572880 | tf_op jit(solution)/shard_map/while/body/eval_jaxpr/all_gather | solution.py:223
  888.0 75.5 %while.59 = (s32[]{:T(128)}, bf16[3,1024,1,64]{1,3,2,0:T(8,128)(2,1)}, bf16[3,2048,1,64]{1,3,2,0:T(8,128)(2,1)}, bf16[3,2048,1,64]{1,3,2,0:T(8,128)(2,1)}, bf16[...) while((s32[]{:T(128)}, ...), condition=%wide.region_21.21_spmd, body=%wide.region_19.20_spmd.sunk | while | flops 1369635840 | bytes 108578080 | solution.py:248
  968.2 24.5 %reduce-scatter.28.cloned.1.call-done = bf16[1024,1,384]{0,2,1:T(8,128)(2,1)} async-done(((bf16[2048,1,384]{0,2,1:T(8,128)(2,1)}), bf16[1024,1,384]{0,2,1:T(8,128)(2,1)}) %reduce-scatter.28.cloned.1.call-update) | async-done | bytes 786448 | tf_op jit(solution)/shard_map/while/body/eval_jaxpr/reduce_scatter | solution.py:271
  1028.7 7.3 convolution_convert_fusion.4
  1037.8 8.4 reduce-scatter.20.cloned.1.call-done
  1048.3 26.3 %reduce-scatter.16.cloned.1.call-done = bf16[192,768]{1,0:T(8,128)(2,1)} async-done(((bf16[768,768]{1,0:T(8,128)(2,1)}), bf16[192,768]{1,0:T(8,128)(2,1)}) %reduce-scatter.16.cloned.1.call-update) | async-done | bytes 294928 | tf_op jit(solution)/shard_map/reduce_scatter | solution.py:302
  1074.6 28.2 %reduce-scatter.18.cloned.1.call-done = bf16[768,192]{0,1:T(8,128)(2,1)} async-done(((bf16[768,768]{0,1:T(8,128)(2,1)}), bf16[768,192]{0,1:T(8,128)(2,1)}) %reduce-scatter.18.cloned.1.call-update) | async-done | bytes 294928 | tf_op jit(solution)/shard_map/reduce_scatter | solution.py:305
  1103.0 8.7 convolution_convert_fusion.1
  1117.6 24.7 %all-reduce.14.cloned.1.call-done = (bf16[3,192,192]{1,2,0:T(8,128)(2,1)}, bf16[192,192]{1,0:T(8,128)(2,1)}, bf16[192,768]{1,0:T(8,128)(2,1)}, bf16[768,192]{0,1:T(8,128)(2,1)}) async-done(((bf16[3,192,192]{1,2,0:T(8,128)(2,1)}, bf16[192,192]{1,0:T(8,128)(2,1)}, bf16[192,768]{1,0:T(8,128)(2,1)}, bf16[768,192]{0,1:T(8,128)(2,1)}), (bf16[3,192,192]{1,2,0:T(8,128)(2,1)}, bf16[192,192]{1,0:T(8,128)(2,1)}, ...) | async-done | bytes 884752 | tf_op jit(solution)/shard_map/psum | solution.py:316
  1149.5 216.3 %all-reduce.12.cloned.1.call-done = (bf16[2048,768]{1,0:T(8,128)(2,1)}, bf16[2048,768]{1,0:T(8,128)(2,1)}) async-done(((bf16[2048,768]{1,0:T(8,128)(2,1)}, bf16[2048,768]{1,0:T(8,128)(2,1)}), (bf16[2048,768]{1,0:T(8,128)(2,1)}, bf16[2048,768]{1,0:T(8,128)(2,1)})) %all-reduce.12.cloned.1.call-update) | async-done | bytes 6291472 | tf_op jit(solution)/shard_map/psum | solution.py:282
  1388.1 8.2 reshape.381
  1411.9 10.4 copy.166
  1424.5 21.2 %reduce-scatter.26.cloned.1.call-done = bf16[192,2]{1,0:T(8,128)(2,1)} async-done(((bf16[768,2]{1,0:T(8,128)(2,1)}), bf16[192,2]{1,0:T(8,128)(2,1)}) %reduce-scatter.26.cloned.1.call-update) | async-done | bytes 784
  (462 shorter events, 446.5 us)
Async XLA Ops:
  8.0 29.6 %copy-start = (bf16[6,2,768]{2,1,0:T(2,128)(2,1)S(1)}, bf16[6,2,768]{2,1,0:T(2,128)(2,1)}, u32[]{:S(2)}) copy-start(bf16[6,2,768]{2,1,0:T(2,128)(2,1)} %param.20) | copy-start | bytes 55300
  8.0 33.4 %copy-start.37 = (s32[1024]{0:T(1024)}, s32[1024]{0:T(1024)S(1)}, u32[]{:S(2)}) copy-start(s32[1024]{0:T(1024)S(1)} %iota_add_fusion.2) | copy-start | bytes 12292
  14.5 28.9 %copy-start.35 = (f32[768]{0:T(1024)}, f32[768]{0:T(1024)S(1)}, u32[]{:S(2)}) copy-start(f32[768]{0:T(1024)S(1)} %get-tuple-element.553) | copy-start | bytes 9220
  21.3 20.1 %copy-start.31 = (f32[1024,2]{0,1:T(2,128)}, f32[1024,2]{0,1:T(2,128)S(1)}, u32[]{:S(2)}) copy-start(f32[1024,2]{0,1:T(2,128)S(1)} %broadcast_subtract_fusion) | copy-start | bytes 24580
  70.7 123.3 %copy-start.39 = (bf16[192,192]{1,0:T(8,128)(2,1)S(1)}, bf16[192,192]{1,0:T(8,128)(2,1)}, u32[]{:S(2)}) copy-start(bf16[192,192]{1,0:T(8,128)(2,1)} %param.24) | copy-start | bytes 221188
  71.2 31.4 %all-gather.11.cloned.1.call-start = ((), (), s32[]{:S(2)}) async-start(), calls=%async_computation.19 | async-start | bytes 2359296 | tf_op jit(solution)/shard_map/while/body/eval_jaxpr/all_gather | solution.py:157
  132.5 30.9 %all-gather.11.cloned.1.call-start = ((), (), s32[]{:S(2)}) async-start(), calls=%async_computation.19 | async-start | bytes 2359296 | tf_op jit(solution)/shard_map/while/body/eval_jaxpr/all_gather | solution.py:157
  193.3 49.8 %all-gather.9.cloned.1.call-start = ((), (), s32[]{:S(2)}) async-start(), calls=%async_computation.9 | async-start | bytes 1474560 | tf_op jit(solution)/shard_map/all_gather | solution.py:119
  193.9 242.5 %all-reduce.8.cloned.1.call-start = ((), (), s32[]{:S(2)}) async-start(), calls=%async_computation.7 | async-start | bytes 12582912 | tf_op jit(solution)/shard_map/psum | solution.py:194
  216.0 230.7 %all-gather.7.cloned.1.call-start = ((), (), s32[]{:S(2)}) async-start(), calls=%async_computation.8 | async-start | bytes 1474560 | tf_op jit(solution)/shard_map/all_gather | solution.py:118
  216.6 468.4 %all-reduce.10.cloned.1.call-start = ((), (), s32[]{:S(2)}) async-start(), calls=%async_computation.10 | async-start | bytes 12582912 | tf_op jit(solution)/shard_map/psum | solution.py:209
  712.7 34.8 %copy-start.5 = (bf16[1024,2,384]{0,2,1:T(8,128)(2,1)}, bf16[1024,2,384]{0,2,1:T(8,128)(2,1)S(1)}, u32[]{:S(2)}) copy-start(bf16[1024,2,384]{0,2,1:T(8,128)(2,1)S(1)} %get-tuple-element.1164) | copy-start | bytes 4718596 | tf_op jit(solution)/shard_map/while
  712.7 34.8 %copy-start.13 = (bf16[1024,2,3,64]{0,3,1,2:T(8,128)(2,1)}, bf16[1024,2,3,64]{0,3,1,2:T(8,128)(2,1)S(1)}, u32[]{:S(2)}) copy-start(bf16[1024,2,3,64]{0,3,1,2:T(8,128)(2,1)S(1)} %get-tuple-element.1163) | copy-start | bytes 2359300 | tf_op jit(solution)/shard_map/while
  712.7 32.1 %all-gather.13.cloned.1.call-start = ((), (), s32[]{:S(2)}) async-start(), calls=%async_computation.20 | async-start | bytes 2359296 | tf_op jit(solution)/shard_map/while/body/eval_jaxpr/all_gather | solution.py:223
  716.4 135.7 %reduce-scatter.28.cloned.1.call-start = ((), (), s32[]{:S(2)}) async-start(), calls=%async_computation.21 | async-start | bytes 2359296 | tf_op jit(solution)/shard_map/while/body/eval_jaxpr/reduce_scatter | solution.py:271
  823.1 31.2 %copy-start.6 = (bf16[1024,2,384]{0,2,1:T(8,128)(2,1)S(1)}, bf16[1024,2,384]{0,2,1:T(8,128)(2,1)}, u32[]{:S(2)}) copy-start(bf16[1024,2,384]{0,2,1:T(8,128)(2,1)} %copy-done.5) | copy-start | bytes 4718596 | tf_op jit(solution)/shard_map/while
  823.1 31.2 %copy-start.14 = (bf16[1024,2,3,64]{0,3,1,2:T(8,128)(2,1)S(1)}, bf16[1024,2,3,64]{0,3,1,2:T(8,128)(2,1)}, u32[]{:S(2)}) copy-start(bf16[1024,2,3,64]{0,3,1,2:T(8,128)(2,1)} %copy-done.13) | copy-start | bytes 2359300 | tf_op jit(solution)/shard_map/while
  854.2 33.8 %copy-start.5 = (bf16[1024,2,384]{0,2,1:T(8,128)(2,1)}, bf16[1024,2,384]{0,2,1:T(8,128)(2,1)S(1)}, u32[]{:S(2)}) copy-start(bf16[1024,2,384]{0,2,1:T(8,128)(2,1)S(1)} %get-tuple-element.1164) | copy-start | bytes 4718596 | tf_op jit(solution)/shard_map/while
  854.2 33.8 %copy-start.13 = (bf16[1024,2,3,64]{0,3,1,2:T(8,128)(2,1)}, bf16[1024,2,3,64]{0,3,1,2:T(8,128)(2,1)S(1)}, u32[]{:S(2)}) copy-start(bf16[1024,2,3,64]{0,3,1,2:T(8,128)(2,1)S(1)} %get-tuple-element.1163) | copy-start | bytes 2359300 | tf_op jit(solution)/shard_map/while
  854.2 31.1 %all-gather.13.cloned.1.call-start = ((), (), s32[]{:S(2)}) async-start(), calls=%async_computation.20 | async-start | bytes 2359296 | tf_op jit(solution)/shard_map/while/body/eval_jaxpr/all_gather | solution.py:223
  858.0 134.7 %reduce-scatter.28.cloned.1.call-start = ((), (), s32[]{:S(2)}) async-start(), calls=%async_computation.21 | async-start | bytes 2359296 | tf_op jit(solution)/shard_map/while/body/eval_jaxpr/reduce_scatter | solution.py:271
  963.5 31.2 %copy-start.6 = (bf16[1024,2,384]{0,2,1:T(8,128)(2,1)S(1)}, bf16[1024,2,384]{0,2,1:T(8,128)(2,1)}, u32[]{:S(2)}) copy-start(bf16[1024,2,384]{0,2,1:T(8,128)(2,1)} %copy-done.5) | copy-start | bytes 4718596 | tf_op jit(solution)/shard_map/while
  963.5 31.2 %copy-start.14 = (bf16[1024,2,3,64]{0,3,1,2:T(8,128)(2,1)S(1)}, bf16[1024,2,3,64]{0,3,1,2:T(8,128)(2,1)}, u32[]{:S(2)}) copy-start(bf16[1024,2,3,64]{0,3,1,2:T(8,128)(2,1)} %copy-done.13) | copy-start | bytes 2359300 | tf_op jit(solution)/shard_map/while
  994.7 41.4 %reduce-scatter.22.cloned.1.call-start = ((), (), s32[]{:S(2)}) async-start(), calls=%async_computation.14 | async-start | bytes 491520
  995.3 50.9 %reduce-scatter.20.cloned.1.call-start = ((), (), s32[]{:S(2)}) async-start(), calls=%async_computation.13 | async-start | bytes 1228800
  1021.8 52.8 %reduce-scatter.16.cloned.1.call-start = ((), (), s32[]{:S(2)}) async-start(), calls=%async_computation.11 | async-start | bytes 1474560 | tf_op jit(solution)/shard_map/reduce_scatter | solution.py:302
  1028.6 74.2 %reduce-scatter.18.cloned.1.call-start = ((), (), s32[]{:S(2)}) async-start(), calls=%async_computation.12 | async-start | bytes 1474560 | tf_op jit(solution)/shard_map/reduce_scatter | solution.py:305
  1036.0 106.3 %all-reduce.14.cloned.1.call-start = ((), (), s32[]{:S(2)}) async-start(), calls=%async_computation.18 | async-start | bytes 1966080 | tf_op jit(solution)/shard_map/psum | solution.py:316
  1102.9 262.8 %all-reduce.12.cloned.1.call-start = ((), (), s32[]{:S(2)}) async-start(), calls=%async_computation.17 | async-start | bytes 12582912 | tf_op jit(solution)/shard_map/psum | solution.py:282
  1115.9 307.7 %reduce-scatter.24.cloned.1.call-start = ((), (), s32[]{:S(2)}) async-start(), calls=%async_computation.15 | async-start | bytes 245760
  1403.1 42.6 %reduce-scatter.26.cloned.1.call-start = ((), (), s32[]{:S(2)}) async-start(), calls=%async_computation.16 | async-start | bytes 245760
  1409.2 45.5 %copy-start.1 = (bf16[6,2,768]{2,1,0:T(2,128)(2,1)S(1)}, bf16[6,2,768]{2,1,0:T(2,128)(2,1)}, u32[]{:S(2)}) copy-start(bf16[6,2,768]{2,1,0:T(2,128)(2,1)} %param.20) | copy-start | bytes 55300
  (80 other events, 343.9 us)
Sparse Core Ops, SparseCore 0:
  74.8 27.6 all-gather.10
  136.1 27.1 all-gather.10
  216.1 220.3 all-reduce.7
  463.1 221.7 all-reduce.9
  716.6 28.2 all-gather.12
  826.1 26.0 reduce-scatter.27
  858.1 27.2 all-gather.12
  966.5 26.0 reduce-scatter.27
  1103.0 39.2 all-reduce.13
  1144.6 221.1 all-reduce.11
Sparse Core Ops, SparseCore 1:
  195.4 19.8 all-gather.8
  218.0 17.3 all-gather.6
  998.3 20.6 reduce-scatter.21
  1021.9 24.3 reduce-scatter.19
  1049.0 25.6 reduce-scatter.15
  1077.2 25.6 reduce-scatter.17
  1403.2 20.4 reduce-scatter.23
  1426.0 19.7 reduce-scatter.25
where the time goes:
time: 1480 us; the launch traced here: 1460 us
  waiting for transfers between devices  884 us (60%)
  matrix products  218 us (15%)
  local copies, waits for them, and re-layouts  176 us (12%)
  other arithmetic  117 us (8%)
  blocking collectives  39.6 us (3%)
  between operations  16.8 us (1%)
    psum x1, waiting for transfers between devices, local(): lax.psum(jnp.einsum('nc,dc->nd', d_projected, qkv_matrix, preferred_eleme...  216 us
    psum x1, waiting for transfers between devices, local(): lax.psum(jnp.einsum('nf,df->nd', d_expanded, fc_full, preferred_element_t...  214 us
    psum x1, waiting for transfers between devices, local(): lax.psum(jnp.dot(attended_b, out_full, preferred_element_type=jnp.float32...  186 us
    dot_general x12, matrix products, score_head(): jnp.einsum('qgd,kgd->gqk', query_head, key_head, preferred_element_type=j...  62.1 us
    all_gather x2, waiting for transfers between devices, forward_block(): lax.all_gather(seq_group(keys_values, block_index, group_size), 'ctx', ax...  53.5 us
    all_gather x2, waiting for transfers between devices, fetch_keys(): lax.all_gather(seq_group(keys_values, block_index, group_size), 'ctx', ax...  53.3 us
    reduce_scatter x2, waiting for transfers between devices, backward_block(): lax.psum_scatter(term.astype(jnp.bfloat16), 'ctx', scatter_dimension=0, t...  48.9 us
    unnamed x106, local copies, waits for them, and re-layouts  48.8 us
  transfers between devices with their start and end apart: 18, of which 15 were waited for; matrix products, arithmetic and copies ran while one was open for 11% of the time, Pallas kernels for 0%

commit v1 on v0

v1 whole, which is shorter than its diff:
```python
import functools

import jax
import jax.numpy as jnp
from jax import lax
from jax.experimental import pallas as pl
from jax.experimental.pallas import tpu as pltpu
from jax.sharding import PartitionSpec as P

HEAD_DIM = 64
DOC_MOST = 1024
EPSILON = 1e-05
MASKED = -1e30


def dot(a, b, dims=((1,), (0,))):
    return lax.dot_general(a, b, (dims, ((), ())), preferred_element_type=jnp.float32)


def hat_rows(values):
    centre = jnp.mean(values, axis=-1, keepdims=True)
    shifted = values - centre
    spread = jnp.mean(shifted * shifted, axis=-1, keepdims=True)
    inv = lax.rsqrt(spread + EPSILON)
    return shifted * inv, inv


def norm_back(hat, inv, gain, grad):
    eg = grad * gain
    return inv * (
        eg
        - jnp.mean(eg, axis=-1, keepdims=True)
        - hat * jnp.mean(eg * hat, axis=-1, keepdims=True)
    )


def attend_kernel(heads, far, block, first_ref, qkv_ref, prev_ref, low_ref, out_ref, out_t_ref, log_ref, k_s, vt_s, qt_s):
    s = pl.program_id(0)
    rows = qkv_ref.shape[0]
    width = heads * HEAD_DIM
    for h in range(heads):
        cols = slice(h * HEAD_DIM, (h + 1) * HEAD_DIM)
        kcols = slice(width + h * HEAD_DIM, width + (h + 1) * HEAD_DIM)
        vcols = slice(2 * width + h * HEAD_DIM, 2 * width + (h + 1) * HEAD_DIM)
        qt_s[h] = (qkv_ref[:, cols].astype(jnp.float32) * 0.125).T.astype(jnp.bfloat16)
        if far:
            k_s[h, : far * rows] = prev_ref[:, cols]
            vt_s[h, :, : far * rows] = prev_ref[:, kcols].astype(jnp.float32).T.astype(jnp.bfloat16)
        k_s[h, far * rows :] = qkv_ref[:, kcols]
        vt_s[h, :, far * rows :] = qkv_ref[:, vcols].astype(jnp.float32).T.astype(jnp.bfloat16)
    for i in range(rows // block):
        span = slice(i * block, (i + 1) * block)
        low = low_ref[:, span]
        top = far * rows + i * block + lax.broadcasted_iota(jnp.int32, (1, block), 1)
        last = far * (rows // block) + i + 1
        for h in range(heads):
            q_t = qt_s[h, :, span]

            def step(kb, carry):
                m, l, acc = carry
                base = pl.multiple_of(kb * block, block)
                scores = dot(k_s[h, pl.ds(base, block), :], q_t)
                place = base + lax.broadcasted_iota(jnp.int32, (block, 1), 0)
                scores = jnp.where((place >= low) & (place <= top), scores, MASKED)
                m_new = jnp.maximum(m, jnp.max(scores, axis=0, keepdims=True))
                p = jnp.exp(scores - m_new)
                alpha = jnp.exp(m - m_new)
                l = alpha * l + jnp.sum(p, axis=0, keepdims=True)
                acc = alpha * acc + dot(vt_s[h, :, pl.ds(base, block)], p.astype(jnp.bfloat16))
                return m_new, l, acc

            m, l, acc = lax.fori_loop(
                first_ref[s, i],
                last,
                step,
                (
                    jnp.full((1, block), MASKED, jnp.float32),
                    jnp.zeros((1, block), jnp.float32),
                    jnp.zeros((HEAD_DIM, block), jnp.float32),
                ),
            )
            mixed = acc / l
            out_t_ref[h * HEAD_DIM : (h + 1) * HEAD_DIM, span] = mixed
            log_ref[h : h + 1, span] = m + jnp.log(l)
        out_ref[span, :] = out_t_ref[:, span].T.astype(jnp.bfloat16)


def attend(qkv, prev, low, first, block):
    seqs, rows, width3 = qkv.shape
    width = width3 // 3
    heads = width // HEAD_DIM
    far = 0 if prev is None else prev.shape[1] // rows
    if prev is None:
        prev = jnp.zeros((seqs, 16, 2 * width), qkv.dtype)
    spec = lambda *shape: pl.BlockSpec((None,) + shape, lambda s, *_: (s, 0, 0))
    return pl.pallas_call(
        functools.partial(attend_kernel, heads, far, block),
        grid_spec=pltpu.PrefetchScalarGridSpec(
            num_scalar_prefetch=1,
            grid=(seqs,),
            in_specs=[spec(rows, width3), spec(prev.shape[1], 2 * width), spec(1, rows)],
            out_specs=[spec(rows, width), spec(width, rows), spec(8, rows)],
            scratch_shapes=[
                pltpu.VMEM((heads, (far + 1) * rows, HEAD_DIM), jnp.bfloat16),
                pltpu.VMEM((heads, HEAD_DIM, (far + 1) * rows), jnp.bfloat16),
                pltpu.VMEM((heads, HEAD_DIM, rows), jnp.bfloat16),
            ],
        ),
        out_shape=[
            jax.ShapeDtypeStruct((seqs, rows, width), jnp.bfloat16),
            jax.ShapeDtypeStruct((seqs, width, rows), jnp.float32),
            jax.ShapeDtypeStruct((seqs, 8, rows), jnp.float32),
        ],
        compiler_params=pltpu.CompilerParams(vmem_limit_bytes=48 << 20),
        cost_estimate=pl.CostEstimate(flops=8 * 10**9, bytes_accessed=8 << 20, transcendentals=8 << 20),
    )(first, qkv, prev, low)


def attend_back_kernel(
    heads, far, block, first_ref, qkv_ref, prev_ref, low_ref, grad_ref, out_t_ref, log_ref,
    dq_ref, dkv_ref, dprev_ref, k_s, kt_s, v_s, q_s, qt_s, g_s, gt_s, dqt_s, dk_s, dv_s,
):
    s = pl.program_id(0)
    rows = qkv_ref.shape[0]
    width = heads * HEAD_DIM
    for h in range(heads):
        cols = slice(h * HEAD_DIM, (h + 1) * HEAD_DIM)
        kcols = slice(width + h * HEAD_DIM, width + (h + 1) * HEAD_DIM)
        vcols = slice(2 * width + h * HEAD_DIM, 2 * width + (h + 1) * HEAD_DIM)
        q = qkv_ref[:, cols].astype(jnp.float32) * 0.125
        q_s[h] = q.astype(jnp.bfloat16)
        qt_s[h] = q.T.astype(jnp.bfloat16)
        g = grad_ref[:, cols]
        g_s[h] = g
        gt_s[h] = g.astype(jnp.float32).T.astype(jnp.bfloat16)
        if far:
            k = prev_ref[:, cols]
            k_s[h, : far * rows] = k
            kt_s[h, :, : far * rows] = k.astype(jnp.float32).T.astype(jnp.bfloat16)
            v_s[h, : far * rows] = prev_ref[:, kcols]
        k = qkv_ref[:, kcols]
        k_s[h, far * rows :] = k
        kt_s[h, :, far * rows :] = k.astype(jnp.float32).T.astype(jnp.bfloat16)
        v_s[h, far * rows :] = qkv_ref[:, vcols]
    dk_s[...] = jnp.zeros_like(dk_s)
    dv_s[...] = jnp.zeros_like(dv_s)
    for i in range(rows // block):
        span = slice(i * block, (i + 1) * block)
        low = low_ref[:, span]
        top = far * rows + i * block + lax.broadcasted_iota(jnp.int32, (1, block), 1)
        last = far * (rows // block) + i + 1
        for h in range(heads):
            cols = slice(h * HEAD_DIM, (h + 1) * HEAD_DIM)
            q_t = qt_s[h, :, span]
            q = q_s[h, span, :]
            g = g_s[h, span, :]
            g_t = gt_s[h, :, span]
            log = log_ref[h : h + 1, span]
            delta = jnp.sum(g_t.astype(jnp.float32) * out_t_ref[cols, span], axis=0, keepdims=True)

            def step(kb, dq_t):
                base = pl.multiple_of(kb * block, block)
                here = pl.ds(base, block)
                scores = dot(k_s[h, here, :], q_t)
                place = base + lax.broadcasted_iota(jnp.int32, (block, 1), 0)
                p = jnp.exp(jnp.where((place >= low) & (place <= top), scores - log, MASKED))
                dp = dot(v_s[h, here, :], g_t)
                ds = (p * (dp - delta)).astype(jnp.bfloat16)
                dv_s[h, here, :] += dot(p.astype(jnp.bfloat16), g)
                dk_s[h, here, :] += dot(ds, q)
                return dq_t + dot(kt_s[h, :, here], ds)

            dqt_s[cols, span] = 0.125 * lax.fori_loop(
                first_ref[s, i], last, step, jnp.zeros((HEAD_DIM, block), jnp.float32)
            )
        dq_ref[span, :] = dqt_s[:, span].T.astype(jnp.bfloat16)
    own = slice(far * rows, (far + 1) * rows)
    dkv_ref[...] = jnp.concatenate(
        [dk_s[h, own] for h in range(heads)] + [dv_s[h, own] for h in range(heads)], axis=1
    )
    if far:
        past = slice(0, far * rows)
        dprev_ref[...] = jnp.concatenate(
            [dk_s[h, past] for h in range(heads)] + [dv_s[h, past] for h in range(heads)], axis=1
        ).astype(jnp.bfloat16)


def attend_back(qkv, prev, low, first, grad, out_t, logs, block):
    seqs, rows, width3 = qkv.shape
    width = width3 // 3
    heads = width // HEAD_DIM
    far = 0 if prev is None else prev.shape[1] // rows
    if prev is None:
        prev = jnp.zeros((seqs, 16, 2 * width), qkv.dtype)
    spec = lambda *shape: pl.BlockSpec((None,) + shape, lambda s, *_: (s, 0, 0))
    span = (far + 1) * rows
    bf, f32 = jnp.bfloat16, jnp.float32
    return pl.pallas_call(
        functools.partial(attend_back_kernel, heads, far, block),
        grid_spec=pltpu.PrefetchScalarGridSpec(
            num_scalar_prefetch=1,
            grid=(seqs,),
            in_specs=[
                spec(rows, width3), spec(prev.shape[1], 2 * width), spec(1, rows),
                spec(rows, width), spec(width, rows), spec(8, rows),
            ],
            out_specs=[spec(rows, width), spec(rows, 2 * width), spec(prev.shape[1], 2 * width)],
            scratch_shapes=[
                pltpu.VMEM((heads, span, HEAD_DIM), bf),
                pltpu.VMEM((heads, HEAD_DIM, span), bf),
                pltpu.VMEM((heads, span, HEAD_DIM), bf),
                pltpu.VMEM((heads, rows, HEAD_DIM), bf),
                pltpu.VMEM((heads, HEAD_DIM, rows), bf),
                pltpu.VMEM((heads, rows, HEAD_DIM), bf),
                pltpu.VMEM((heads, HEAD_DIM, rows), bf),
                pltpu.VMEM((width, rows), f32),
                pltpu.VMEM((heads, span, HEAD_DIM), f32),
                pltpu.VMEM((heads, span, HEAD_DIM), f32),
            ],
        ),
        out_shape=[
            jax.ShapeDtypeStruct((seqs, rows, width), bf),
            jax.ShapeDtypeStruct((seqs, rows, 2 * width), f32),
            jax.ShapeDtypeStruct((seqs, prev.shape[1], 2 * width), bf),
        ],
        compiler_params=pltpu.CompilerParams(vmem_limit_bytes=56 << 20),
        cost_estimate=pl.CostEstimate(flops=16 * 10**9, bytes_accessed=16 << 20, transcendentals=8 << 20),
    )(first, qkv, prev, low, grad, out_t, logs)


def local(
    inputs, thoughts, positions, lengths, w_qkv, w_out, w_fc, w_proj, norm_gains, norm_biases, out_grad,
):
    rows, seqs, width = inputs.shape
    ctx_count = lax.axis_size("ctx")
    tp_count = lax.axis_size("tp")
    ctx, tp = lax.axis_index("ctx"), lax.axis_index("tp")
    first_row = ctx * rows
    own_rows = rows // tp_count
    own_tokens = own_rows * seqs
    far = min(ctx_count - 1, -(-(DOC_MOST - 1) // rows))
    block = min(256, rows)
    bf, f32 = jnp.bfloat16, jnp.float32

    qkv_full = lax.all_gather(w_qkv, "fsdp", axis=1, tiled=True)
    params = lax.all_gather(jnp.concatenate([norm_gains, norm_biases]), "fsdp", axis=1, tiled=True).astype(f32)
    gains, biases = params[:2], params[2:]
    everywhere = lambda w, axes: functools.reduce(
        lambda v, pair: lax.all_gather(v, pair[0], axis=pair[1], tiled=True), axes, w
    )
    out_full = everywhere(w_out, (("tp", 0), ("fsdp", 1)))
    fc_full = everywhere(w_fc, (("tp", 1), ("fsdp", 0)))
    proj_full = everywhere(w_proj, (("tp", 0), ("fsdp", 1)))
    qkv_all = everywhere(w_qkv, (("tp", 2), ("fsdp", 1)))

    local_width = qkv_full.shape[2]
    qkv_matrix = jnp.transpose(qkv_full, (1, 0, 2)).reshape(width, 3 * local_width)
    places = first_row + jnp.arange(rows, dtype=jnp.int32)
    is_thought = places[None, None, :] == positions[:, :, None]
    keep = jnp.logical_not(jnp.any(is_thought, axis=0))
    start = jnp.transpose(inputs, (1, 0, 2))
    for t in range(thoughts.shape[0]):
        start = jnp.where(is_thought[t][:, :, None], thoughts[t][:, None, :], start)
    hat, inv = hat_rows(start.astype(f32))
    normed = (hat * gains[0] + biases[0]).astype(bf)
    normed_flat = normed.reshape(seqs * rows, width)
    qkv = dot(normed_flat, qkv_matrix).astype(bf).reshape(seqs, rows, 3 * local_width)

    ends = jnp.cumsum(lengths, axis=1, dtype=jnp.int32)
    low = jnp.max(jnp.where(ends[:, :, None] <= places[None, None, :], ends[:, :, None], 0), axis=1)
    low = low - (first_row - far * rows)
    first = low[:, ::block] // block

    kv = qkv[:, :, local_width:]
    prev = None
    if far:
        prev = jnp.concatenate(
            [
                lax.ppermute(kv, "ctx", [(i, i + d) for i in range(ctx_count - d)])
                for d in range(far, 0, -1)
            ],
            axis=1,
        )
    low3 = low[:, None, :]
    attended, out_t, logs = attend(qkv, prev, low3, first, block)

    own = lambda a: lax.dynamic_slice_in_dim(a, tp * own_rows, own_rows, 1).reshape(own_tokens, width)
    spread = lambda a: lax.all_to_all(a, "tp", split_axis=1, concat_axis=2, tiled=True).reshape(own_tokens, -1)
    attended_own = spread(attended)
    start_own = own(start).astype(f32)
    grad_own = jnp.transpose(
        lax.dynamic_slice_in_dim(out_grad, tp * own_rows, own_rows, 0), (1, 0, 2)
    ).reshape(own_tokens, width)
    middle = start_own + dot(attended_own, out_full)
    mid_hat, mid_inv = hat_rows(middle)
    normed_mid = (mid_hat * gains[1] + biases[1]).astype(bf)
    expanded = dot(normed_mid, fc_full)
    act, gelu_back = jax.vjp(lambda v: jax.nn.gelu(v, approximate=True), expanded)
    activated = act.astype(bf)
    output_own = (middle + dot(activated, proj_full)).astype(bf)
    d_activated = dot(grad_own, proj_full, ((1,), (1,)))
    d_expanded = gelu_back(d_activated)[0].astype(bf)
    d_normed_mid = dot(d_expanded, fc_full, ((1,), (1,)))
    d_middle = grad_own.astype(f32) + norm_back(mid_hat, mid_inv, gains[1], d_normed_mid)
    d_middle_b = d_middle.astype(bf)
    d_attended_own = dot(d_middle_b, out_full, ((1,), (1,))).astype(bf)
    d_attended = lax.all_to_all(
        d_attended_own.reshape(seqs, own_rows, width), "tp", split_axis=2, concat_axis=1, tiled=True
    )
    output = lax.all_gather(output_own.reshape(seqs, own_rows, width), "tp", axis=1, tiled=True)
    output = jnp.transpose(output, (1, 0, 2))
    d_proj = dot(activated, grad_own, ((0,), (0,)))
    d_fc = dot(normed_mid, d_expanded, ((0,), (0,)))
    d_out = dot(attended_own, d_middle_b, ((0,), (0,)))

    d_q, d_kv, d_prev = attend_back(qkv, prev, low3, first, d_attended, out_t, logs, block)
    for index, d in enumerate(range(far, 0, -1)):
        piece = d_prev[:, index * rows : (index + 1) * rows]
        d_kv = d_kv + lax.ppermute(piece, "ctx", [(i + d, i) for i in range(ctx_count - d)]).astype(f32)
    d_qkv = jnp.concatenate([d_q, d_kv.astype(bf)], axis=2)
    d_w_qkv = dot(normed_flat, d_qkv.reshape(seqs * rows, -1), ((0,), (0,)))
    d_w_qkv = jnp.transpose(d_w_qkv.reshape(width, 3, local_width), (1, 0, 2))
    d_qkv_own = lax.all_to_all(d_qkv, "tp", split_axis=1, concat_axis=2, tiled=True)
    d_qkv_own = d_qkv_own.reshape(own_tokens, tp_count, 3, local_width)
    qkv_all = qkv_all.reshape(3, width, tp_count, local_width)
    d_normed = lax.dot_general(
        d_qkv_own, qkv_all, (((1, 2, 3), (2, 0, 3)), ((), ())), preferred_element_type=f32
    )
    hat_own, inv_own = hat_rows(start_own)
    d_start_own = d_middle + norm_back(hat_own, inv_own, gains[0], d_normed)
    d_start = lax.all_gather(d_start_own.astype(bf).reshape(seqs, own_rows, width), "tp", axis=1, tiled=True)
    d_inputs = jnp.transpose(jnp.where(keep[:, :, None], d_start.astype(f32), 0.0), (1, 0, 2))
    d_thoughts = jnp.einsum(
        "tsr,srd->tsd", is_thought.astype(bf), d_start, preferred_element_type=f32
    )
    small = jnp.stack(
        [
            jnp.sum(d_normed * hat_own, axis=0),
            jnp.sum(d_normed_mid * mid_hat, axis=0),
            jnp.sum(d_normed, axis=0),
            jnp.sum(d_normed_mid, axis=0),
        ]
    )
    reduce = lambda g, axes: lax.psum(
        functools.reduce(
            lambda v, pair: lax.psum_scatter(v, pair[0], scatter_dimension=pair[1], tiled=True),
            axes,
            g.astype(bf),
        ),
        "ctx",
    ).astype(f32)
    small = lax.psum(lax.psum_scatter(small, "fsdp", scatter_dimension=1, tiled=True), ("ctx", "tp"))
    return (
        output,
        d_inputs,
        lax.psum(d_thoughts.astype(bf), "ctx").astype(f32),
        reduce(d_w_qkv, (("fsdp", 1),)),
        reduce(d_out, (("fsdp", 1), ("tp", 0))),
        reduce(d_fc, (("fsdp", 0), ("tp", 1))),
        reduce(d_proj, (("fsdp", 1), ("tp", 0))),
        small[:2],
        small[2],
        small[3],
    )


def solution(mesh):
    in_specs = (
        P("ctx", "fsdp", None),
        P(None, "fsdp", None),
        P(None, "fsdp"),
        P("fsdp", None),
        P(None, "fsdp", "tp"),
        P("tp", "fsdp"),
        P("fsdp", "tp"),
        P("tp", "fsdp"),
        P(None, "fsdp"),
        P(None, "fsdp"),
        P("ctx", "fsdp", None),
    )
    out_specs = (
        P("ctx", "fsdp", None),
        P("ctx", "fsdp", None),
        P(None, "fsdp", None),
        P(None, "fsdp", "tp"),
        P("tp", "fsdp"),
        P("fsdp", "tp"),
        P("tp", "fsdp"),
        P(None, "fsdp"),
        P("fsdp"),
        P("fsdp"),
    )
    return jax.shard_map(local, mesh=mesh, in_specs=in_specs, out_specs=out_specs, check_vma=False)
```

time: 1480 us -> 777 us (0.53)
  waiting for transfers between devices: 884 us -> 358 us
  matrix products: 218 us -> 68 us
  other arithmetic: 117 us -> 34.1 us
  local copies, waits for them, and re-layouts: 176 us -> 104 us
  blocking collectives: 39.6 us -> 105 us
  Pallas kernels: 0 us -> 60 us
  starting transfers between devices: 1.31 us -> 22.4 us
    psum x4 -> x1, waiting for transfers between devices: 641 us -> 20 us  [local(): lax.psum(functools.reduce(lambda v, pair: lax.psum_scatter(v, pair[0], sc...]
    dot_general x56 -> x13, matrix products: 218 us -> 68 us  [the longest x11 61.3 us: dot(): lax.dot_general(a, b, (dims, ((), ())), preferred_element_type=jnp.float32)]
    all_to_all x0 -> x2, waiting for transfers between devices: none -> 94.6 us  [the longest x1 74.9 us: local(): lax.all_to_all(d_qkv, 'tp', split_axis=1, concat_axis=2, tiled=True)]
    ppermute x0 -> x2, waiting for transfers between devices: none -> 79.4 us  [the longest x1 47.4 us: local(): lax.ppermute(piece, 'ctx', [(i + d, i) for i in range(ctx_count - d)])]
    pallas_call x0 -> x2, Pallas kernels: none -> 60 us  [the longest x1 32.6 us: attend_back(): pl.pallas_call(functools.partial(attend_back_kernel, heads, far, block),...]
    reduce_scatter x4 -> x5, waiting for transfers between devices: 103 us -> 44.7 us  [local(): lax.psum_scatter(v, pair[0], scatter_dimension=pair[1], tiled=True)]
    convert_element_type x16 -> x5, other arithmetic: 55.3 us -> 10.6 us  [the longest x2 3.63 us: local(): reduce = lambda g, axes: lax.psum(functools.reduce(lambda v, pair: lax.ps...]
    all_gather x4, blocking collectives: 33.3 us -> 61.7 us  [the longest x2 42.2 us: local(): lax.all_gather(v, pair[0], axis=pair[1], tiled=True)]
  transfers between devices with their start and end apart: 18 -> 21, of which waited for: 15 -> 11; matrix products, arithmetic and copies ran while one was open for 11% -> 22% of each run, Pallas kernels for 0% -> 8%
where the time goes in v1:
time: 777 us; the launch traced here: 765 us
  waiting for transfers between devices  358 us (46%)
  blocking collectives  105 us (14%)
  local copies, waits for them, and re-layouts  104 us (13%)
  matrix products  68 us (9%)
  Pallas kernels  60 us (8%)
  other arithmetic  34.1 us (4%)
  starting transfers between devices  22.4 us (3%)
  between operations  14.7 us (2%)
    all_to_all x1, waiting for transfers between devices, local(): lax.all_to_all(d_qkv, 'tp', split_axis=1, concat_axis=2, tiled=True)  74.9 us
    all_gather x1, waiting for transfers between devices, local(): lax.all_gather(d_start_own.astype(bf).reshape(seqs, own_rows, width), 'tp...  63.2 us
    dot_general x11, matrix products, dot(): lax.dot_general(a, b, (dims, ((), ())), preferred_element_type=jnp.float32)  61.3 us
    ppermute x1, waiting for transfers between devices, local(): lax.ppermute(piece, 'ctx', [(i + d, i) for i in range(ctx_count - d)])  47.4 us
    reduce_scatter x5, waiting for transfers between devices, local(): lax.psum_scatter(v, pair[0], scatter_dimension=pair[1], tiled=True)  44.7 us
    all_gather x2, blocking collectives, local(): lax.all_gather(v, pair[0], axis=pair[1], tiled=True)  42.2 us
    unnamed x67, local copies, waits for them, and re-layouts  42.1 us
    pallas_call x1, Pallas kernels, attend_back(): pl.pallas_call(functools.partial(attend_back_kernel, heads, far, block),...  32.6 us
  transfers between devices with their start and end apart: 21, of which 11 were waited for; matrix products, arithmetic and copies ran while one was open for 22% of the time, Pallas kernels for 8%

profile of v1, /device:TPU:25, one launch (start us, length us, event | category | flops | bytes accessed | tf_op | source)
XLA Modules:
  0.0 765.3 jit_solution(4717519656084596435)
XLA Ops:
  8.8 14.0 %all_gather.38 = bf16[768,192]{1,0:T(8,128)(2,1)S(1)} all-gather(bf16[192,192]{1,0:T(8,128)(2,1)} %param.16), channel_id=1, replica_groups=mesh['fsdp'=4,'ctx'=2,'tp'=4] {'tp'}, dimensions={0}, use_global_device_ids=true | all-gather | bytes 368640 | tf_op jit(solution)/shard_map/all_gather | solution.py:249
  23.7 17.2 %all-gather.16.cloned.1.call-done = bf16[3072,192]{0,1:T(8,128)(2,1)} async-done(((bf16[768,192]{0,1:T(8,128)(2,1)}), bf16[3072,192]{0,1:T(8,128)(2,1)}) %all-gather.16.cloned.1.call-update) | async-done | bytes 1179664 | tf_op jit(solution)/shard_map/all_gather | solution.py:249
  51.4 9.5 %convert_reduce_fusion = (f32[2,1024]{1,0:T(2,128)}, bf16[2,1024,768]{2,1,0:T(8,128)(2,1)}) fusion(bf16[1024,2,768]{2,1,0:T(2,128)(2,1)} %param.11, bf16[2,768]{1,0:T(2,128)(2,1)S(1)} %get-tuple-element.102, pred[2,1024]{1,0:T(4,128)(4,1)S(1)} %get-tuple-element.93, bf16[2,768]{1,0:T(2,128)(2,1)S(1)} %get-tuple-element.103, ...), kind=kLoop, calls=%fused_computation.3 | loop fusion | flops 12580864 | bytes 6330368 | tf_op jit(solution)/shard_map/reduce_sum | solution.py:21
  60.9 10.9 %all-gather.12.cloned.1.call-done = bf16[192,3072]{1,0:T(8,128)(2,1)} async-done(((bf16[192,768]{1,0:T(8,128)(2,1)}), bf16[192,3072]{1,0:T(8,128)(2,1)}) %all-gather.12.cloned.1.call-update) | async-done | bytes 1179664 | tf_op jit(solution)/shard_map/all_gather | solution.py:249
  71.9 13.9 %all_gather.37 = bf16[3,768,192]{2,0,1:T(4,128)(2,1)} all-gather(bf16[3,192,192]{2,0,1:T(4,128)(2,1)S(1)} %copy.110), channel_id=1, replica_groups=mesh['fsdp'=4,'ctx'=2,'tp'=4] {'fsdp'}, dimensions={1}, use_global_device_ids=true | all-gather | bytes 1105920 | tf_op jit(solution)/shard_map/all_gather | solution.py:245
  112.7 32.0 %collective-permute-done.prev_ref = bf16[2,1024,384]{2,1,0:T(8,128)(2,1)} collective-permute-done((bf16[2,1024,384]{2,1,0:T(8,128)(2,1)}, bf16[2,1024,384]{2,1,0:T(8,128)(2,1)}, u32[]{:S(2)}, u32[]{:S(2)}) %collective-permute-start) | collective-permute-done | bytes 1572896 | tf_op jit(solution)/shard_map/ppermute | solution.py:279
  144.7 27.4 %shard_map.186 = (bf16[2,1024,192]{2,1,0:T(8,128)(2,1)S(1)}, f32[2,192,1024]{2,1,0:T(8,128)S(1)}, f32[2,8,1024]{2,1,0:T(8,128)S(1)}) custom-call(s32[2,4]{1,0:T(2,128)S(1)} %and_select_fusion.first_ref, bf16[2,1024,576]{2,1,0:T(8,128)(2,1)} %bitcast.157, bf16[2,1024,384]{2,1,0:T(8,128)(2,1)} %collective-permute-done.prev_ref, s32[2,1,1024]{2,1,0:T(1,128)S(1)} %sub.83.low_ref), custom_call_target="tpu_custom_call" | custom-call | flops 8000000000 | bytes 8388608 | tf_op jit(solution)/shard_map/pallas_call | solution.py:96
  176.0 7.7 %all-to-all-start = ((bf16[2,1024,192]{2,0,1:T(2,128)(2,1)}), bf16[2,1024,192]{2,0,1:T(2,128)(2,1)}, u32[]{:S(2)}, u32[]{:S(2)}) async-start(bf16[2,1024,192]{2,0,1:T(2,128)(2,1)} %copy.113), calls=%async_computation | async-start | bytes 2097152 | tf_op jit(solution)/shard_map/all_to_all | solution.py:288
  187.0 19.7 %all-to-all-done = bf16[2,1024,192]{2,0,1:T(2,128)(2,1)} async-done(((bf16[2,1024,192]{2,0,1:T(2,128)(2,1)}), bf16[2,1024,192]{2,0,1:T(2,128)(2,1)}, u32[]{:S(2)}, u32[]{:S(2)}) %all-to-all-start) | async-done | bytes 786464 | tf_op jit(solution)/shard_map/all_to_all | solution.py:288
  214.3 7.0 fusion.44
  221.3 11.9 %fusion.12 = (bf16[512,3072]{1,0:T(8,128)(2,1)S(1)}, f32[512,3072]{1,0:T(8,128)}) fusion(f32[512,3072]{1,0:T(8,128)} %fusion.44, bf16[768,3072]{1,0:T(8,128)(2,1)} %all-gather.14.cloned.1.call-done, f32[512,768]{1,0:T(8,128)S(1)} %get-tuple-element.109, f32[768]{0:T(1024)S(1)} %get-tuple-element.81, f32[768]{0:T(1024)S(1)} %get-tuple-element.80, ...), kind=kOutput, calls=%fused_computation.16 | convolution fusion | flops 2449342464 | bytes 22030336 | tf_op jit(solution)/shard_map/dot_general | solution.py:17
  240.6 28.2 %all_gather.45 = bf16[3,192,768]{1,0,2:T(4,128)(2,1)} all-gather(bf16[3,192,192]{1,0,2:T(4,128)(2,1)S(1)} %copy.123), channel_id=1, replica_groups=mesh['fsdp'=4,'ctx'=2,'tp'=4] {'tp'}, dimensions={2}, use_global_device_ids=true | all-gather | bytes 1105920 | tf_op jit(solution)/shard_map/all_gather | solution.py:249
  272.5 7.4 convolution_convert_fusion.1
  280.0 8.0 %convolution_convert_fusion = bf16[3072,768]{0,1:T(8,128)(2,1)} fusion(bf16[512,768]{1,0:T(8,128)(2,1)S(1)} %bitcast.155, f32[512,3072]{1,0:T(8,128)} %get-tuple-element.111), kind=kOutput, calls=%fused_computation.19 | convolution fusion | flops 2432434176 | bytes 11796480 | tf_op jit(solution)/shard_map/dot_general | solution.py:17
  290.9 21.5 %all_to_all.48 = bf16[2,256,768]{1,0,2:T(2,128)(2,1)S(1)} all-to-all(bf16[2,256,768]{1,0,2:T(2,128)(2,1)S(1)} %copy.118), channel_id=1, replica_groups=mesh['fsdp'=4,'ctx'=2,'tp'=4] {'tp'}, dimensions={2} | all-to-all | bytes 1572864 | tf_op jit(solution)/shard_map/all_to_all | solution.py:307
  313.8 32.6 %shard_map.187 = (bf16[2,1024,192]{2,1,0:T(8,128)(2,1)}, f32[2,1024,384]{2,1,0:T(8,128)}, bf16[2,1024,384]{2,1,0:T(8,128)(2,1)}) custom-call(s32[2,4]{1,0:T(2,128)} %copy-done.3, bf16[2,1024,576]{2,1,0:T(8,128)(2,1)} %bitcast.158, bf16[2,1024,384]{2,1,0:T(8,128)(2,1)} %collective-permute-done.prev_ref, s32[2,1,1024]{2,1,0:T(1,128)} %copy-done.2, ...), custom_call_target="tpu_custom_call" | custom-call | flops 16000000000 | bytes 16777216 | tf_op jit(solution)/shard_map/pallas_call | solution.py:198
  349.9 47.4 %collective-permute-done.1 = bf16[2,1024,384]{2,1,0:T(8,128)(2,1)S(1)} collective-permute-done((bf16[2,1024,384]{2,1,0:T(8,128)(2,1)}, bf16[2,1024,384]{2,1,0:T(8,128)(2,1)S(1)}, u32[]{:S(2)}, u32[]{:S(2)}) %collective-permute-start.1) | collective-permute-done | bytes 1572896 | tf_op jit(solution)/shard_map/ppermute | solution.py:319
  416.6 8.4 %add_convert_fusion.1 = bf16[512,768]{1,0:T(8,128)(2,1)S(1)} fusion(f32[512,768]{1,0:T(8,128)} %copy-done.10, bf16[3072,768]{0,1:T(8,128)(2,1)} %all-gather.18.cloned.1.call-done, f32[512,3072]{1,0:T(8,128)} %get-tuple-element.111), kind=kOutput, calls=%fused_computation.53 | convolution fusion | flops 2430861312 | bytes 13369344 | tf_op jit(solution)/shard_map/dot_general | solution.py:17
  431.0 7.3 all-to-all-start.2
  438.9 6.0 copy.125
  444.9 74.9 %all-to-all-done.2 = bf16[2,1024,576]{2,0,1:T(2,128)(2,1)} async-done(((bf16[2,1024,576]{2,0,1:T(2,128)(2,1)}), bf16[2,1024,576]{2,0,1:T(2,128)(2,1)}, u32[]{:S(2)}, u32[]{:S(2)}) %all-to-all-start.2) | async-done | bytes 2359328 | tf_op jit(solution)/shard_map/all_to_all | solution.py:323
  519.9 10.9 %copy.122 = bf16[2,4,256,576]{2,0,3,1:T(2,128)(2,1)} copy(bf16[2,4,256,576]{3,0,2,1:T(2,128)(2,1)} %bitcast.31) | data formatting | bytes 4718592 | tf_op jit(solution)/shard_map/all_to_all | solution.py:323
  530.8 6.4 reshape.173
  537.2 6.2 fusion.20
  552.9 25.0 %reduce-scatter.29.cloned.1.call-done = f32[192,4]{1,0:T(8,128)} async-done(((f32[768,4]{1,0:T(8,128)}), f32[192,4]{1,0:T(8,128)}) %reduce-scatter.29.cloned.1.call-update) | async-done | bytes 3088
  578.9 13.9 %psum.47 = f32[4,192]{1,0:T(4,128)S(1)} all-reduce(f32[4,192]{1,0:T(4,128)S(1)} %copy.139), channel_id=1, replica_groups=mesh['fsdp'=4,'ctx'=2,'tp'=4] {'ctx','tp'}, use_global_device_ids=true, to_apply=%region_30.31 | all-reduce | flops 768 | bytes 6144 | tf_op jit(solution)/shard_map/psum | solution.py:352
  592.8 14.7 %reduce-scatter.19.cloned.1.call-done = bf16[192,768]{1,0:T(8,128)(2,1)} async-done(((bf16[192,3072]{1,0:T(8,128)(2,1)}), bf16[192,768]{1,0:T(8,128)(2,1)}) %reduce-scatter.19.cloned.1.call-update) | async-done | bytes 294928 | tf_op jit(solution)/shard_map/reduce_scatter | solution.py:346
  607.5 30.0 %reduce-scatter.23.cloned.1.call-done = bf16[768,192]{0,1:T(8,128)(2,1)} async-done(((bf16[3072,192]{0,1:T(8,128)(2,1)}), bf16[768,192]{0,1:T(8,128)(2,1)}) %reduce-scatter.23.cloned.1.call-update) | async-done | bytes 294928 | tf_op jit(solution)/shard_map/reduce_scatter | solution.py:346
  638.7 63.2 %all-gather.24.cloned.1.call-done = bf16[2,1024,768]{2,1,0:T(8,128)(2,1)} async-done(((bf16[2,256,768]{2,1,0:T(8,128)(2,1)}), bf16[2,1024,768]{2,1,0:T(8,128)(2,1)}) %all-gather.24.cloned.1.call-update) | async-done | bytes 3145744 | tf_op jit(solution)/shard_map/all_gather | solution.py:331
  706.2 10.5 %copy.129 = f32[1024,2,768]{2,1,0:T(2,128)} copy(f32[1024,2,768]{2,0,1:T(8,128)} %select_bitcast_fusion) | data formatting | bytes 12582912
  717.2 7.6 psum.42
  725.5 20.0 %all-reduce.3.cloned.1.call-done = (bf16[3,192,192]{1,2,0:T(8,128)(2,1)}, bf16[192,192]{0,1:T(8,128)(2,1)}, bf16[192,768]{1,0:T(8,128)(2,1)}, bf16[768,192]{0,1:T(8,128)(2,1)}) async-done(((bf16[3,192,192]{1,2,0:T(8,128)(2,1)}, bf16[192,192]{0,1:T(8,128)(2,1)}, bf16[192,768]{1,0:T(8,128)(2,1)}, bf16[768,192]{0,1:T(8,128)(2,1)}), (bf16[3,192,192]{1,2,0:T(8,128)(2,1)}, bf16[192,192]{0,1:T(8,128)(2,1)}, ...) | async-done | bytes 884752 | tf_op jit(solution)/shard_map/psum | solution.py:344
  (180 shorter events, 129.1 us)
Async XLA Ops:
  7.2 177.1 %copy-start = (bf16[1024,2,768]{2,1,0:T(2,128)(2,1)S(1)}, bf16[1024,2,768]{2,1,0:T(2,128)(2,1)}, u32[]{:S(2)}) copy-start(bf16[1024,2,768]{2,1,0:T(2,128)(2,1)} %param.21) | copy-start | bytes 9437188
  7.2 33.8 %copy-start.18 = (s32[6,2]{0,1:T(2,128)S(1)}, s32[6,2]{0,1:T(2,128)}, u32[]{:S(2)}) copy-start(s32[6,2]{0,1:T(2,128)} %param.13) | copy-start | bytes 148
  7.2 34.5 %copy-start.21 = (bf16[2,192]{1,0:T(2,128)(2,1)S(1)}, bf16[2,192]{1,0:T(2,128)(2,1)}, u32[]{:S(2)}) copy-start(bf16[2,192]{1,0:T(2,128)(2,1)} %param.19) | copy-start | bytes 2308
  7.2 34.5 %copy-start.20 = (bf16[2,192]{1,0:T(2,128)(2,1)S(1)}, bf16[2,192]{1,0:T(2,128)(2,1)}, u32[]{:S(2)}) copy-start(bf16[2,192]{1,0:T(2,128)(2,1)} %param.20) | copy-start | bytes 2308
  7.2 33.7 %all-gather.16.cloned.1.call-start = ((), (), s32[]{:S(2)}) async-start(), calls=%async_computation.14 | async-start | bytes 1474560 | tf_op jit(solution)/shard_map/all_gather | solution.py:249
  8.0 63.9 %all-gather.12.cloned.1.call-start = ((), (), s32[]{:S(2)}) async-start(), calls=%async_computation.12 | async-start | bytes 1474560 | tf_op jit(solution)/shard_map/all_gather | solution.py:249
  8.7 202.9 %all-gather.10.cloned.1.call-start = ((), (), s32[]{:S(2)}) async-start(), calls=%async_computation.11 | async-start | bytes 1474560 | tf_op jit(solution)/shard_map/all_gather | solution.py:249
  23.7 190.7 %all-gather.18.cloned.1.call-start = ((), (), s32[]{:S(2)}) async-start(), calls=%async_computation.15 | async-start | bytes 5898240 | tf_op jit(solution)/shard_map/all_gather | solution.py:249
  40.9 180.4 %all-gather.14.cloned.1.call-start = ((), (), s32[]{:S(2)}) async-start(), calls=%async_computation.13 | async-start | bytes 5898240 | tf_op jit(solution)/shard_map/all_gather | solution.py:249
  99.5 12.7 %copy-start.19 = (s32[2,3]{1,0:T(2,128)S(1)}, s32[2,3]{1,0:T(2,128)}, u32[]{:S(2)}) copy-start(s32[2,3]{1,0:T(2,128)} %param.14) | copy-start | bytes 76
  107.6 37.0 %collective-permute-start = (bf16[2,1024,384]{2,1,0:T(8,128)(2,1)}, bf16[2,1024,384]{2,1,0:T(8,128)(2,1)}, u32[]{:S(2)}, u32[]{:S(2)}) collective-permute-start(bf16[2,1024,384]{2,1,0:T(8,128)(2,1)} %slice.100), channel_id=1, source_target_pairs={{0,4},{1,5},{2,6},{3,7},{8,12},{9,13},{10,14},{11,15},{16,20},{17,... | collective-permute-start | bytes 4718600 | tf_op jit(solution)/shard_map/ppermute | solution.py:279
  112.6 59.5 %copy-start.2 = (s32[2,1,1024]{2,1,0:T(1,128)}, s32[2,1,1024]{2,1,0:T(1,128)S(1)}, u32[]{:S(2)}) copy-start(s32[2,1,1024]{2,1,0:T(1,128)S(1)} %sub.83.low_ref) | copy-start | bytes 24580
  112.7 59.4 %copy-start.3 = (s32[2,4]{1,0:T(2,128)}, s32[2,4]{1,0:T(2,128)S(1)}, u32[]{:S(2)}) copy-start(s32[2,4]{1,0:T(2,128)S(1)} %and_select_fusion.first_ref) | copy-start | bytes 100
  176.0 30.6 %all-to-all-start = ((bf16[2,1024,192]{2,0,1:T(2,128)(2,1)}), bf16[2,1024,192]{2,0,1:T(2,128)(2,1)}, u32[]{:S(2)}, u32[]{:S(2)}) async-start(bf16[2,1024,192]{2,0,1:T(2,128)(2,1)} %copy.113), calls=%async_computation | async-start | bytes 2097152 | tf_op jit(solution)/shard_map/all_to_all | solution.py:288
  183.7 164.0 %reduce-scatter.15.cloned.1.call-start = ((), (), s32[]{:S(2)}) async-start(), calls=%async_computation.19 | async-start | bytes 1474560 | tf_op jit(solution)/shard_map/reduce_scatter | solution.py:346
  214.0 19.2 %copy-start.10 = (f32[512,768]{1,0:T(8,128)}, f32[512,768]{1,0:T(8,128)S(1)}, u32[]{:S(2)}) copy-start(f32[512,768]{1,0:T(8,128)S(1)} %get-tuple-element.109) | copy-start | bytes 4718596
  221.3 11.9 %copy-start.22 = (bf16[768,3072]{1,0:T(8,128)(2,1)S(1)}, bf16[768,3072]{1,0:T(8,128)(2,1)}, u32[]{:S(2)}) copy-start(bf16[768,3072]{1,0:T(8,128)(2,1)} %all-gather.14.cloned.1.call-done) | copy-start | bytes 14155780
  238.3 49.8 %copy-start.8 = (f32[512,768]{1,0:T(8,128)}, f32[512,768]{1,0:T(8,128)S(1)}, u32[]{:S(2)}) copy-start(f32[512,768]{1,0:T(8,128)S(1)} %multiply_add_fusion) | copy-start | bytes 4718596
  240.3 198.7 %all-gather.22.cloned.1.call-start = ((), (), s32[]{:S(2)}) async-start(), calls=%async_computation.17 | async-start | bytes 4423680 | tf_op jit(solution)/shard_map/all_gather | solution.py:249
  272.3 272.2 %reduce-scatter.17.cloned.1.call-start = ((), (), s32[]{:S(2)}) async-start(), calls=%async_computation.20 | async-start | bytes 5898240 | tf_op jit(solution)/shard_map/reduce_scatter | solution.py:346
  280.0 265.1 %reduce-scatter.21.cloned.1.call-start = ((), (), s32[]{:S(2)}) async-start(), calls=%async_computation.22 | async-start | bytes 5898240 | tf_op jit(solution)/shard_map/reduce_scatter | solution.py:346
  288.1 261.1 %reduce-scatter.27.cloned.1.call-start = ((), (), s32[]{:S(2)}) async-start(), calls=%async_computation.25 | async-start | bytes 491520
  346.4 50.9 %collective-permute-start.1 = (bf16[2,1024,384]{2,1,0:T(8,128)(2,1)}, bf16[2,1024,384]{2,1,0:T(8,128)(2,1)S(1)}, u32[]{:S(2)}, u32[]{:S(2)}) collective-permute-start(bf16[2,1024,384]{2,1,0:T(8,128)(2,1)} %get-tuple-element.21), channel_id=1, source_target_pairs={{4,0},{5,1},{6,2},{7,3},{12,8},{13,9},{14,10},{15,11},{20,16},{21,... | collective-permute-start | bytes 4718600 | tf_op jit(solution)/shard_map/ppermute | solution.py:319
  349.6 201.1 %reduce-scatter.25.cloned.1.call-start = ((), (), s32[]{:S(2)}) async-start(), calls=%async_computation.24 | async-start | bytes 1228800
  416.6 136.3 %all-gather.20.cloned.1.call-start = ((), (), s32[]{:S(2)}) async-start(), calls=%async_computation.16 | async-start | bytes 3932160 | tf_op jit(solution)/shard_map/all_gather | solution.py:310
  431.0 88.9 %all-to-all-start.2 = ((bf16[2,1024,576]{2,0,1:T(2,128)(2,1)}), bf16[2,1024,576]{2,0,1:T(2,128)(2,1)}, u32[]{:S(2)}, u32[]{:S(2)}) async-start(bf16[2,1024,576]{2,0,1:T(2,128)(2,1)} %copy.121), calls=%async_computation.2 | async-start | bytes 5242880 | tf_op jit(solution)/shard_map/all_to_all | solution.py:323
  438.3 139.6 %reduce-scatter.29.cloned.1.call-start = ((), (), s32[]{:S(2)}) async-start(), calls=%async_computation.26 | async-start | bytes 491520
  544.4 63.1 %reduce-scatter.19.cloned.1.call-start = ((), (), s32[]{:S(2)}) async-start(), calls=%async_computation.21 | async-start | bytes 1474560 | tf_op jit(solution)/shard_map/reduce_scatter | solution.py:346
  545.0 92.5 %reduce-scatter.23.cloned.1.call-start = ((), (), s32[]{:S(2)}) async-start(), calls=%async_computation.23 | async-start | bytes 1474560 | tf_op jit(solution)/shard_map/reduce_scatter | solution.py:346
  545.6 156.2 %all-gather.24.cloned.1.call-start = ((), (), s32[]{:S(2)}) async-start(), calls=%async_computation.18 | async-start | bytes 3932160 | tf_op jit(solution)/shard_map/all_gather | solution.py:331
  549.0 196.5 %all-reduce.3.cloned.1.call-start = ((), (), s32[]{:S(2)}) async-start(), calls=%async_computation.27 | async-start | bytes 1966080 | tf_op jit(solution)/shard_map/psum | solution.py:344
  706.2 10.5 %copy-start.16 = (pred[6,2,1024]{2,1,0:T(4,128)(4,1)S(1)}, pred[6,2,1024]{2,1,0:T(4,128)(4,1)}, u32[]{:S(2)}) copy-start(pred[6,2,1024]{2,1,0:T(4,128)(4,1)} %copy-done.15) | copy-start | bytes 36868
  (13 other events, 45.9 us)
Sparse Core Ops, SparseCore 0:
  9.6 31.2 all-gather.15
  42.5 29.3 all-gather.11
  74.0 18.8 all-gather.9
  94.3 37.4 all-gather.17
  133.2 37.4 all-gather.13
  240.4 35.2 reduce-scatter.14
  277.3 36.3 all-gather.21
  316.4 47.4 reduce-scatter.16
  366.4 47.8 reduce-scatter.20
  417.1 16.7 reduce-scatter.26
  436.5 35.4 reduce-scatter.24
  473.5 73.9 all-gather.19
  550.7 27.1 reduce-scatter.28
  580.2 27.2 reduce-scatter.18
  609.8 27.6 reduce-scatter.22
  639.6 62.2 all-gather.23
  704.9 40.5 all-reduce.2

commit v2 on v1

v2 whole, which is shorter than its diff:
```python
import functools

import jax
import jax.numpy as jnp
from jax import lax
from jax.experimental import pallas as pl
from jax.experimental.pallas import tpu as pltpu
from jax.sharding import PartitionSpec as P

HEAD_DIM = 64
DOC_MOST = 1024
EPSILON = 1e-05
MASKED = -1e30


def dot(a, b, dims=((1,), (0,))):
    return lax.dot_general(a, b, (dims, ((), ())), preferred_element_type=jnp.float32)


def hat_rows(values):
    centre = jnp.mean(values, axis=-1, keepdims=True)
    shifted = values - centre
    spread = jnp.mean(shifted * shifted, axis=-1, keepdims=True)
    inv = lax.rsqrt(spread + EPSILON)
    return shifted * inv, inv


def norm_back(hat, inv, gain, grad):
    eg = grad * gain
    return inv * (
        eg
        - jnp.mean(eg, axis=-1, keepdims=True)
        - hat * jnp.mean(eg * hat, axis=-1, keepdims=True)
    )


MESH = pl.DeviceIdType.MESH
VMEM_LIMIT = 60 << 20


def column(index, size=HEAD_DIM):
    return slice(index * size, (index + 1) * size)


def turn(value):
    return value.astype(jnp.float32).T.astype(jnp.bfloat16)


def attend_kernel(heads, far, block, first_ref, qkv_ref, prev_ref, low_ref, out_ref, out_t_ref, log_ref, k_s, vt_s, qt_s):
    s = pl.program_id(0)
    rows = qkv_ref.shape[0]
    parts, own_rows = out_ref.shape[0], out_ref.shape[1]
    for h in range(heads):
        qt_s[h] = turn(qkv_ref[:, column(h)].astype(jnp.float32) * 0.125)
        if far:
            k_s[h, : far * rows] = prev_ref[:, column(h)]
            vt_s[h, :, : far * rows] = turn(prev_ref[:, column(heads + h)])
        k_s[h, far * rows :] = qkv_ref[:, column(heads + h)]
        vt_s[h, :, far * rows :] = turn(qkv_ref[:, column(2 * heads + h)])
    for i in range(rows // block):
        span = column(i, block)
        low = low_ref[:, span]
        top = far * rows + i * block + lax.broadcasted_iota(jnp.int32, (1, block), 1)
        last = far * (rows // block) + i + 1

        def step(kb, carry):
            base = pl.multiple_of(kb * block, block)
            here = pl.ds(base, block)
            place = base + lax.broadcasted_iota(jnp.int32, (block, 1), 0)
            allowed = (place >= low) & (place <= top)
            after = []
            for h in range(heads):
                m, l, acc = carry[h]
                scores = dot(k_s[h, here, :], qt_s[h, :, span])
                scores = jnp.where(allowed, scores, MASKED)
                m_new = jnp.maximum(m, jnp.max(scores, axis=0, keepdims=True))
                p = jnp.exp(scores - m_new)
                alpha = jnp.exp(m - m_new)
                l = alpha * l + jnp.sum(p, axis=0, keepdims=True)
                acc = alpha * acc + dot(vt_s[h, :, here], p.astype(jnp.bfloat16))
                after.append((m_new, l, acc))
            return tuple(after)

        ends = lax.fori_loop(
            first_ref[s, i],
            last,
            step,
            tuple(
                (
                    jnp.full((1, block), MASKED, jnp.float32),
                    jnp.zeros((1, block), jnp.float32),
                    jnp.zeros((HEAD_DIM, block), jnp.float32),
                )
                for _ in range(heads)
            ),
        )
        for h, (m, l, acc) in enumerate(ends):
            out_t_ref[column(h), span] = acc / l
            log_ref[h : h + 1, span] = m + jnp.log(l)
    for t in range(parts):
        out_ref[t] = turn_back(out_t_ref[:, column(t, own_rows)])


def turn_back(value):
    return value.T.astype(jnp.bfloat16)


def attend(qkv, prev, low, first, block, parts):
    seqs, rows, width3 = qkv.shape
    width = width3 // 3
    heads = width // HEAD_DIM
    far = 0 if prev is None else prev.shape[1] // rows
    if prev is None:
        prev = jnp.zeros((seqs, 16, 2 * width), qkv.dtype)
    spec = lambda *shape: pl.BlockSpec((None,) + shape, lambda s, *_: (s, 0, 0))
    return pl.pallas_call(
        functools.partial(attend_kernel, heads, far, block),
        grid_spec=pltpu.PrefetchScalarGridSpec(
            num_scalar_prefetch=1,
            grid=(seqs,),
            in_specs=[spec(rows, width3), spec(prev.shape[1], 2 * width), spec(1, rows)],
            out_specs=[
                pl.BlockSpec((parts, None, rows // parts, width), lambda s, *_: (0, s, 0, 0)),
                spec(width, rows),
                spec(8, rows),
            ],
            scratch_shapes=[
                pltpu.VMEM((heads, (far + 1) * rows, HEAD_DIM), jnp.bfloat16),
                pltpu.VMEM((heads, HEAD_DIM, (far + 1) * rows), jnp.bfloat16),
                pltpu.VMEM((heads, HEAD_DIM, rows), jnp.bfloat16),
            ],
        ),
        out_shape=[
            jax.ShapeDtypeStruct((parts, seqs, rows // parts, width), jnp.bfloat16),
            jax.ShapeDtypeStruct((seqs, width, rows), jnp.float32),
            jax.ShapeDtypeStruct((seqs, 8, rows), jnp.float32),
        ],
        compiler_params=pltpu.CompilerParams(vmem_limit_bytes=48 << 20),
        cost_estimate=pl.CostEstimate(flops=8 * 10**9, bytes_accessed=8 << 20, transcendentals=8 << 20),
    )(first, qkv, prev, low)


def attend_back_kernel(
    heads, far, block, first_ref, qkv_ref, prev_ref, low_ref, grad_ref, out_t_ref, log_ref,
    dq_ref, dkv_ref, dprev_ref, k_s, kt_s, v_s, q_s, qt_s, g_s, gt_s, dqt_s, dk_s, dv_s,
):
    s = pl.program_id(0)
    rows = qkv_ref.shape[0]
    parts, own_rows = grad_ref.shape[0], grad_ref.shape[1]
    for h in range(heads):
        q = qkv_ref[:, column(h)].astype(jnp.float32) * 0.125
        q_s[h] = q.astype(jnp.bfloat16)
        qt_s[h] = turn_back(q)
        for t in range(parts):
            g_s[h, column(t, own_rows), :] = grad_ref[t, :, column(h)]
        gt_s[h] = turn(g_s[h])
        if far:
            k = prev_ref[:, column(h)]
            k_s[h, : far * rows] = k
            kt_s[h, :, : far * rows] = turn(k)
            v_s[h, : far * rows] = prev_ref[:, column(heads + h)]
        k = qkv_ref[:, column(heads + h)]
        k_s[h, far * rows :] = k
        kt_s[h, :, far * rows :] = turn(k)
        v_s[h, far * rows :] = qkv_ref[:, column(2 * heads + h)]
    dk_s[...] = jnp.zeros_like(dk_s)
    dv_s[...] = jnp.zeros_like(dv_s)
    for i in range(rows // block):
        span = column(i, block)
        low = low_ref[:, span]
        top = far * rows + i * block + lax.broadcasted_iota(jnp.int32, (1, block), 1)
        last = far * (rows // block) + i + 1
        deltas = [
            jnp.sum(gt_s[h, :, span].astype(jnp.float32) * out_t_ref[column(h), span], axis=0, keepdims=True)
            for h in range(heads)
        ]

        def step(kb, carry):
            base = pl.multiple_of(kb * block, block)
            here = pl.ds(base, block)
            place = base + lax.broadcasted_iota(jnp.int32, (block, 1), 0)
            allowed = (place >= low) & (place <= top)
            after = []
            for h in range(heads):
                scores = dot(k_s[h, here, :], qt_s[h, :, span])
                p = jnp.exp(jnp.where(allowed, scores - log_ref[h : h + 1, span], MASKED))
                dp = dot(v_s[h, here, :], gt_s[h, :, span])
                ds = (p * (dp - deltas[h])).astype(jnp.bfloat16)
                dv_s[h, here, :] += dot(p.astype(jnp.bfloat16), g_s[h, span, :])
                dk_s[h, here, :] += dot(ds, q_s[h, span, :])
                after.append(carry[h] + dot(kt_s[h, :, here], ds))
            return tuple(after)

        ends = lax.fori_loop(
            first_ref[s, i], last, step, tuple(jnp.zeros((HEAD_DIM, block), jnp.float32) for _ in range(heads))
        )
        for h in range(heads):
            dqt_s[column(h), span] = 0.125 * ends[h]
    for t in range(parts):
        dq_ref[t] = dqt_s[:, column(t, own_rows)].astype(jnp.bfloat16)
    for h in range(heads):
        for source, at in ((dk_s, h), (dv_s, heads + h)):
            whole = source[h].T
            for d in range(far):
                for t in range(parts):
                    dprev_ref[d, t, column(at), :] = whole[:, column(d * parts + t, own_rows)].astype(jnp.bfloat16)
            for t in range(parts):
                dkv_ref[t, column(at), :] = whole[:, column(far * parts + t, own_rows)]


def attend_back(qkv, prev, low, first, grad, out_t, logs, block):
    seqs, rows, width3 = qkv.shape
    parts = grad.shape[0]
    own_rows = rows // parts
    width = width3 // 3
    heads = width // HEAD_DIM
    far = 0 if prev is None else prev.shape[1] // rows
    if prev is None:
        prev = jnp.zeros((seqs, 16, 2 * width), qkv.dtype)
    spec = lambda *shape: pl.BlockSpec((None,) + shape, lambda s, *_: (s, 0, 0))
    chunked = lambda *shape: pl.BlockSpec((parts, None) + shape, lambda s, *_: (0, s, 0, 0))
    span = (far + 1) * rows
    dists = max(far, 1)
    bf, f32 = jnp.bfloat16, jnp.float32
    return pl.pallas_call(
        functools.partial(attend_back_kernel, heads, far, block),
        grid_spec=pltpu.PrefetchScalarGridSpec(
            num_scalar_prefetch=1,
            grid=(seqs,),
            in_specs=[
                spec(rows, width3), spec(prev.shape[1], 2 * width), spec(1, rows),
                chunked(own_rows, width), spec(width, rows), spec(8, rows),
            ],
            out_specs=[
                chunked(width, own_rows), chunked(2 * width, own_rows),
                pl.BlockSpec((dists, parts, None, 2 * width, own_rows), lambda s, *_: (0, 0, s, 0, 0)),
            ],
            scratch_shapes=[
                pltpu.VMEM((heads, span, HEAD_DIM), bf),
                pltpu.VMEM((heads, HEAD_DIM, span), bf),
                pltpu.VMEM((heads, span, HEAD_DIM), bf),
                pltpu.VMEM((heads, rows, HEAD_DIM), bf),
                pltpu.VMEM((heads, HEAD_DIM, rows), bf),
                pltpu.VMEM((heads, rows, HEAD_DIM), bf),
                pltpu.VMEM((heads, HEAD_DIM, rows), bf),
                pltpu.VMEM((width, rows), f32),
                pltpu.VMEM((heads, span, HEAD_DIM), f32),
                pltpu.VMEM((heads, span, HEAD_DIM), f32),
            ],
        ),
        out_shape=[
            jax.ShapeDtypeStruct((parts, seqs, width, own_rows), bf),
            jax.ShapeDtypeStruct((parts, seqs, 2 * width, own_rows), f32),
            jax.ShapeDtypeStruct((dists, parts, seqs, 2 * width, own_rows), bf),
        ],
        compiler_params=pltpu.CompilerParams(vmem_limit_bytes=VMEM_LIMIT),
        cost_estimate=pl.CostEstimate(flops=16 * 10**9, bytes_accessed=16 << 20, transcendentals=8 << 20),
    )(first, qkv, prev, low, grad, out_t, logs)


def feed_kernel(
    step_cols, att_ref, start_ref, grad_ref, out_w_ref, params_ref, fc_ref, proj_ref,
    out_ref, datt_ref, dmid_ref, g_ref, small_ref,
    mid_s, nm_s, nmt_s, gt_s, acc_s, dnm_s, stage_s, last_s, sems, last_sem,
):
    t = pl.program_id(0)
    parts = pl.num_programs(0)
    count = att_ref.shape[0]
    part_cols = att_ref.shape[2]
    shards = stage_s.shape[1]
    shard_rows = stage_s.shape[2]
    hidden = fc_ref.shape[1]
    bf, f32 = jnp.bfloat16, jnp.float32

    @pl.when(t == 0)
    def _():
        mid = start_ref[...].astype(f32)
        for c in range(count):
            mid = mid + dot(att_ref[c], out_w_ref[column(c, part_cols), :])
        mid_s[...] = mid
        hat, _ = hat_rows(mid)
        nm = hat * params_ref[1:2] + params_ref[3:4]
        nm_s[...] = nm.astype(bf)
        nmt_s[...] = turn_back(nm)
        gt_s[...] = turn(grad_ref[...])
        acc_s[...] = jnp.zeros_like(acc_s)
        dnm_s[...] = jnp.zeros_like(dnm_s)

    slot = lax.rem(t, 2)
    store = lambda at, where: pltpu.make_async_copy(
        stage_s.at[where], g_ref.at[:, at, :, pl.ds(0, 2 * hidden)], sems.at[where]
    )

    @pl.when(t >= 2)
    def _():
        store(t - 2, slot).wait()

    def one(j, _):
        here = pl.ds(pl.multiple_of(j * step_cols, step_cols), step_cols)
        there = pl.ds(pl.multiple_of(hidden + j * step_cols, step_cols), step_cols)
        fc = fc_ref[:, here]
        proj = proj_ref[:, here]
        x = dot(nm_s[...], fc)
        d_act = dot(grad_ref[...], proj)
        square = x * x
        th = jnp.tanh(0.7978845608028654 * (x + 0.044715 * (square * x)))
        half = 0.5 * (1.0 + th)
        act = (x * half).astype(bf)
        slope = half + (0.5 * x) * (1.0 - th * th) * (
            0.7978845608028654 * (1.0 + (3 * 0.044715) * square)
        )
        d_exp = (slope * d_act).astype(bf)
        acc_s[...] += dot(act, proj, ((1,), (1,)))
        dnm_s[...] += dot(d_exp, fc, ((1,), (1,)))
        d_fc = dot(nmt_s[...], d_exp).astype(bf)
        d_proj = dot(gt_s[...], act).astype(bf)
        for f in range(shards):
            stage_s[slot, f, :, here] = d_fc[column(f, shard_rows)]
            stage_s[slot, f, :, there] = d_proj[column(f, shard_rows)]
        return 0

    lax.fori_loop(0, hidden // step_cols, one, 0)
    store(t, slot).start()

    @pl.when(t == parts - 1)
    def _():
        mid = mid_s[...]
        out_ref[...] = (mid + acc_s[...]).astype(bf)
        hat, inv = hat_rows(mid)
        d_nm = dnm_s[...]
        d_mid = grad_ref[...].astype(f32) + norm_back(hat, inv, params_ref[1:2], d_nm)
        dmid_ref[...] = d_mid
        d_mid_b = d_mid.astype(bf)
        d_mid_t = turn_back(d_mid)
        small_ref[...] = jnp.concatenate(
            [
                jnp.zeros((1, mid.shape[1]), f32),
                jnp.sum(d_nm * hat, axis=0, keepdims=True),
                jnp.zeros((1, mid.shape[1]), f32),
                jnp.sum(d_nm, axis=0, keepdims=True),
                jnp.zeros((4, mid.shape[1]), f32),
            ],
            axis=0,
        )
        for c in range(count):
            datt_ref[c] = dot(d_mid_b, out_w_ref[column(c, part_cols), :], ((1,), (1,))).astype(bf)
            d_out = dot(d_mid_t, att_ref[c]).astype(bf)
            for f in range(shards):
                last_s[f, c, :, :part_cols] = d_out[column(f, shard_rows)]
        if last_s.shape[3] > part_cols:
            last_s[:, :, :, part_cols:] = jnp.zeros(last_s.shape[:3] + (last_s.shape[3] - part_cols,), bf)
        final = pltpu.make_async_copy(
            last_s, g_ref.at[:, :, :, pl.ds(2 * hidden, last_s.shape[3])], last_sem
        )
        final.start()
        if parts >= 2:
            store(parts - 2, (parts - 2) % 2).wait()
        store(parts - 1, (parts - 1) % 2).wait()
        final.wait()


def padded(size):
    return -(-size // 128) * 128


def feed(att, start, grad, out_w, params, fc, proj_t, shards):
    parts, tokens, part_cols = att.shape
    width, hidden_all = fc.shape
    hidden = hidden_all // parts
    shard_rows = width // shards
    step_cols = 256
    wide = 2 * hidden + padded(part_cols)
    bf, f32 = jnp.bfloat16, jnp.float32
    whole = lambda *shape: pl.BlockSpec(shape, lambda t: (0,) * len(shape))
    return pl.pallas_call(
        functools.partial(feed_kernel, step_cols),
        grid=(parts,),
        in_specs=[
            whole(parts, tokens, part_cols), whole(tokens, width), whole(tokens, width), whole(width, width),
            whole(4, width),
            pl.BlockSpec((width, hidden), lambda t: (0, t)),
            pl.BlockSpec((width, hidden), lambda t: (0, t)),
        ],
        out_specs=[
            whole(tokens, width), whole(parts, tokens, part_cols), whole(tokens, width),
            pl.BlockSpec(memory_space=pl.ANY), whole(8, width),
        ],
        out_shape=[
            jax.ShapeDtypeStruct((tokens, width), bf),
            jax.ShapeDtypeStruct((parts, tokens, part_cols), bf),
            jax.ShapeDtypeStruct((tokens, width), f32),
            jax.ShapeDtypeStruct((shards, parts, shard_rows, wide), bf),
            jax.ShapeDtypeStruct((8, width), f32),
        ],
        scratch_shapes=[
            pltpu.VMEM((tokens, width), f32),
            pltpu.VMEM((tokens, width), bf),
            pltpu.VMEM((width, tokens), bf),
            pltpu.VMEM((width, tokens), bf),
            pltpu.VMEM((tokens, width), f32),
            pltpu.VMEM((tokens, width), f32),
            pltpu.VMEM((2, shards, shard_rows, 2 * hidden), bf),
            pltpu.VMEM((shards, parts, shard_rows, padded(part_cols)), bf),
            pltpu.SemaphoreType.DMA((2,)),
            pltpu.SemaphoreType.DMA,
        ],
        compiler_params=pltpu.CompilerParams(vmem_limit_bytes=VMEM_LIMIT),
        cost_estimate=pl.CostEstimate(flops=17 * 10**9, bytes_accessed=40 << 20, transcendentals=2 << 20),
    )(att, start, grad, out_w, params, fc, proj_t)


def add_rows(target, sources, rows_at_once=16):
    def one(i, _):
        here = pl.ds(pl.multiple_of(i * rows_at_once, rows_at_once), rows_at_once)
        total = target[here, :].astype(jnp.float32)
        for source in sources:
            total = total + source[here, :].astype(jnp.float32)
        target[here, :] = total.astype(target.dtype)
        return 0

    lax.fori_loop(0, target.shape[0] // rows_at_once, one, 0)


def finish_kernel(
    sizes,
    dq_ref, dkv_ref, rec_ref, normed_ref, wall_ref, g_ref, start_ref, dmid_ref, gain_ref, small_in, pick_ref,
    dstart_ref, gw_ref, gq_ref, small_ref,
    kv_s, rq, rkv, normed_s, wall_s, own_g, rcore, rx, rc, rz, gq_acc, gq_s, rgq, rb, rgc,
    dst_s, sm_s, rst, rsc, rsf,
    core_sem, core_rec, x_sem, x_rec, c_sem, c_rec, z_sem, z_rec, b_sem, b_rec,
    aq_sem, aq_rec, ak_sem, ak_rec, ag_sem, ag_rec, gq_sem, gq_rec, gc_sem, gc_rec,
    st_sem, st_rec, sc_sem, sc_rec, sf_sem, sf_rec, loc_sem, own_sem,
):
    F, C, T = sizes
    f, c, t = lax.axis_index("fsdp"), lax.axis_index("ctx"), lax.axis_index("tp")
    S = dq_ref.shape[1]
    part = dq_ref.shape[2]
    own_rows = dq_ref.shape[3]
    bf, f32 = jnp.bfloat16, jnp.float32
    sib, across, opposite = f ^ 1, f ^ 2, f ^ 3

    def remote(src, dst, send, recv, **where):
        return pltpu.make_async_remote_copy(
            src_ref=src, dst_ref=dst, send_sem=send, recv_sem=recv, device_id=where, device_id_type=MESH
        )

    locals_ = []
    for tt in range(T):
        for ff in range(F):
            locals_.append(
                pltpu.make_async_copy(
                    wall_ref.at[tt, ff],
                    wall_s.at[tt, :, pl.ds(ff * part, part), :],
                    loc_sem.at[2 + tt * F + ff],
                )
            )
    normed_in = pltpu.make_async_copy(normed_ref, normed_s, loc_sem.at[0])
    g_in = [
        pltpu.make_async_copy(g_ref.at[f], own_g.at[0], own_sem.at[0]),
        pltpu.make_async_copy(g_ref.at[across], own_g.at[1], own_sem.at[1]),
    ]
    for copy in g_in:
        copy.start()
    normed_in.start()
    for copy in locals_:
        copy.start()

    barrier = pltpu.get_barrier_semaphore()
    peers = 0
    for d in range(1, F):
        pl.semaphore_signal(barrier, inc=1, device_id={"fsdp": f ^ d}, device_id_type=MESH)
        peers += 1
    for d in range(1, T):
        pl.semaphore_signal(barrier, inc=1, device_id={"tp": lax.rem(t + d, T)}, device_id_type=MESH)
        peers += 1
    for d in range(1, C):
        pl.semaphore_signal(barrier, inc=1, device_id={"ctx": lax.rem(c + d, C)}, device_id_type=MESH)
        peers += 1
    pl.semaphore_wait(barrier, peers)

    def tp_peer(d):
        return lax.rem(t + d, T)

    pending = []

    def go(copy):
        copy.start()
        pending.append(copy)
        return copy

    aq = [[None] * S for _ in range(T)]
    ak = [[None] * S for _ in range(T)]
    for s in range(S):
        for d in range(1, T):
            aq[d][s] = go(
                remote(dq_ref.at[tp_peer(d), s], rq.at[d, s], aq_sem.at[d, s], aq_rec.at[d, s], tp=tp_peer(d))
            )
    core = [[None, None] for _ in range(T)]
    for b in range(T):
        for k, target in enumerate((sib, opposite)):
            core[b][k] = go(
                remote(g_ref.at[target, b], rcore.at[b, k], core_sem.at[b, k], core_rec.at[b, k], fsdp=sib)
            )
    for s in range(S):
        for d in list(range(1, T)) + [0]:
            peer = tp_peer(d)
            kv_s[d, s] = (dkv_ref[peer, s] + rec_ref[peer, s].astype(f32)).astype(bf)
            if d:
                ak[d][s] = go(
                    remote(kv_s.at[d, s], rkv.at[d, s], ak_sem.at[d, s], ak_rec.at[d, s], tp=peer)
                )

    for copy in g_in:
        copy.wait()
    cross = [None] * T
    for b in range(T):
        core[b][1].wait_recv()
        add_rows(own_g.at[1, b], [rcore.at[b, 1]])
        cross[b] = go(remote(own_g.at[1, b], rx.at[b], x_sem.at[b], x_rec.at[b], fsdp=across))
        core[b][0].wait_recv()
        add_rows(own_g.at[0, b], [rcore.at[b, 0]])

    normed_in.wait()
    gq_acc[...] = jnp.zeros_like(gq_acc)
    for s in range(S):
        for d in range(T):
            peer = tp_peer(d)
            rows = pl.ds(pl.multiple_of(peer * own_rows, own_rows), own_rows)
            gq_acc[:part, :] += dot(dq_ref[peer, s], normed_s[s, rows, :])
            gq_acc[part:, :] += dot(kv_s[d, s], normed_s[s, rows, :])
    for k in range(F):
        gq_s[k] = gq_acc[:, column(k, part)].astype(bf)
    gq = [None] * F
    for d in range(1, F):
        gq[d] = go(remote(gq_s.at[f ^ d], rgq.at[d], gq_sem.at[d], gq_rec.at[d], fsdp=f ^ d))

    held = [b // C for b in range(T)]

    def ctx_stage(b):
        owner = b % C
        cross[b].wait_recv()
        add_rows(own_g.at[0, b], [rx.at[b]])
        for d in range(1, C):
            @pl.when(lax.rem(c + d, C) == owner)
            def _():
                remote(
                    own_g.at[0, b], rc.at[held[b], d], c_sem.at[b], c_rec.at[b, d], ctx=owner
                ).start()

    def ctx_wait(b):
        owner = b % C

        @pl.when(c == owner)
        def _():
            for d in range(1, C):
                remote(own_g.at[0, b], rc.at[held[b], d], c_sem.at[b], c_rec.at[b, d], ctx=owner).wait_recv()
            add_rows(own_g.at[0, b], [rc.at[held[b], d] for d in range(1, C)])

    def z_stage(b):
        owner = b % C

        def hop(step, way):
            return remote(
                own_g.at[0, b], rz.at[held[b], way], z_sem.at[b], z_rec.at[b, way], tp=t + step
            )

        @pl.when(c == owner)
        def _():
            if b < T - 1:
                @pl.when((t >= b) & (t < T - 1))
                def _():
                    hop(-1, 0).wait_recv()
                    add_rows(own_g.at[0, b], [rz.at[held[b], 0]])

                @pl.when(t > b)
                def _():
                    hop(-1, 0).start()
            if b > 0:
                @pl.when((t <= b) & (t > 0))
                def _():
                    hop(1, 1).wait_recv()
                    add_rows(own_g.at[0, b], [rz.at[held[b], 1]])

                @pl.when(t < b)
                def _():
                    hop(1, 1).start()

    hat, inv = [None] * S, [None] * S
    gain = gain_ref[...]

    def norm_stage(s):
        total = jnp.zeros((wall_s.shape[2], own_rows), f32)
        for d in range(T):
            if d:
                aq[d][s].wait_recv()
                ak[d][s].wait_recv()
            source = lax.rem(t + T - d, T)
            for j in range(3):
                if d:
                    block = rq[d, s] if j == 0 else rkv[d, s, column(j - 1, part), :]
                else:
                    block = dq_ref[t, s] if j == 0 else kv_s[0, s, column(j - 1, part), :]
                total = total + dot(wall_s[source, j], block)
        d_normed = total.T
        hat, inv = hat_rows(start_ref[s].astype(f32))
        value = dmid_ref[s] + norm_back(hat, inv, gain, d_normed)
        dst_s[s] = value.astype(bf)
        return (
            jnp.sum(d_normed * hat, axis=0, keepdims=True),
            jnp.sum(d_normed, axis=0, keepdims=True),
        )

    def ag_copy(s, owner, step, way):
        rows = pl.ds(pl.multiple_of(owner * own_rows, own_rows), own_rows)
        src = dst_s.at[s] if step == 0 else dstart_ref.at[s, rows, :]
        return lambda to: remote(
            src, dstart_ref.at[s, rows, :], ag_sem.at[s, step, way], ag_rec.at[s, step, way], tp=to
        )

    def ag_start(s):
        @pl.when(t < T - 1)
        def _():
            ag_copy(s, t, 0, 0)(t + 1).start()

        @pl.when(t > 0)
        def _():
            ag_copy(s, t, 0, 1)(t - 1).start()

        rows = pl.ds(pl.multiple_of(t * own_rows, own_rows), own_rows)
        keep = pltpu.make_async_copy(dst_s.at[s], dstart_ref.at[s, rows, :], loc_sem.at[1])
        keep.start()
        keep.wait()

    def ag_step(s, step):
        @pl.when(t >= step)
        def _():
            ag_copy(s, t - step, step - 1, 0)(t).wait_recv()

        @pl.when((t >= step) & (t < T - 1))
        def _():
            ag_copy(s, t - step, step, 0)(t + 1).start()

        @pl.when(t + step <= T - 1)
        def _():
            ag_copy(s, t + step, step - 1, 1)(t).wait_recv()

        @pl.when((t + step <= T - 1) & (t > 0))
        def _():
            ag_copy(s, t + step, step, 1)(t - 1).start()

    def ag_drain(s):
        for step in range(T - 1):
            @pl.when((t >= step) & (t < T - 1))
            def _():
                ag_copy(s, t - step, step, 0)(t + 1).wait_send()

            @pl.when((t + step <= T - 1) & (t > 0))
            def _():
                ag_copy(s, t + step, step, 1)(t - 1).wait_send()

    for copy in locals_:
        copy.wait()
    sums = [None] * S
    for s in range(S):
        for b in range(s * T // S, (s + 1) * T // S):
            ctx_stage(b)
        sums[s] = norm_stage(s)
        ag_start(s)
    gain_sum = sum(pair[0] for pair in sums)
    bias_sum = sum(pair[1] for pair in sums)
    sm_s[0:8, :] = small_in[...] + jnp.concatenate(
        [gain_sum, jnp.zeros_like(gain_sum), bias_sum, jnp.zeros((5, gain_sum.shape[1]), f32)], axis=0
    )
    thoughts = jnp.zeros((pick_ref.shape[1], sm_s.shape[1]), f32)
    for s in range(S):
        thoughts = thoughts + dot(pick_ref[s], dst_s[s])
    sm_s[8:, :] = thoughts
    st = [None] * T
    for d in range(1, T):
        st[d] = go(remote(sm_s, rst.at[d], st_sem.at[d], st_rec.at[d], tp=tp_peer(d)))

    gq_sum = gq_s[f].astype(f32)
    for d in range(1, F):
        gq[d].wait_recv()
        gq_sum = gq_sum + rgq[d].astype(f32)
    rgc[c] = gq_sum.astype(bf)
    gc = [None] * C
    for d in range(1, C):
        gc[d] = go(remote(rgc.at[c], rgc.at[c], gc_sem.at[d], gc_rec.at[d], ctx=lax.rem(c + d, C)))

    for b in range(T):
        ctx_wait(b)
        z_stage(b)
    for step in range(1, T):
        for s in range(S):
            ag_step(s, step)

    for d in range(1, T):
        st[d].wait_recv()
    rst[0] = sm_s[...]
    total = jnp.zeros(sm_s.shape, f32)
    for k in range(T):
        total = total + rst[lax.rem(t + T - k, T)]
    rsc[c] = total
    sc = [None] * C
    for d in range(1, C):
        sc[d] = go(remote(rsc.at[c], rsc.at[c], sc_sem.at[d], sc_rec.at[d], ctx=lax.rem(c + d, C)))
    for d in range(1, C):
        sc[d].wait_recv()
    total = jnp.zeros(sm_s.shape, f32)
    for k in range(C):
        total = total + rsc[k]
    rsf[f] = total
    sf = [None] * F
    for d in range(1, F):
        sf[d] = go(remote(rsf.at[f], rsf.at[f], sf_sem.at[d], sf_rec.at[d], fsdp=f ^ d))
    for d in range(1, F):
        sf[d].wait_recv()
    norms = jnp.zeros((8, sm_s.shape[1]), f32)
    for k in range(F):
        norms = norms + rsf[k, 0:8, :]
    small_ref[0:8, :] = norms
    small_ref[8:, :] = total[8:]

    for d in range(1, C):
        gc[d].wait_recv()
    total = jnp.zeros(gq_ref.shape, f32)
    for k in range(C):
        total = total + rgc[k].astype(f32)
    gq_ref[...] = total

    for b in range(T):
        owner = b % C

        @pl.when((t == b) & (c == owner))
        def _():
            for d in range(1, C):
                remote(
                    own_g.at[0, b], rb, b_sem.at[d], b_rec, ctx=lax.rem(owner + d, C)
                ).start()
            gw_ref[...] = own_g[0, b]
            for d in range(1, C):
                remote(
                    own_g.at[0, b], rb, b_sem.at[d], b_rec, ctx=lax.rem(owner + d, C)
                ).wait_send()

        @pl.when((t == b) & (c != owner))
        def _():
            remote(own_g.at[0, b], rb, b_sem.at[1], b_rec, ctx=owner).wait_recv()
            gw_ref[...] = rb[...]

    for copy in pending:
        copy.wait_send()
    for b in range(T):
        owner = b % C

        @pl.when(c != owner)
        def _():
            remote(own_g.at[0, b], rc.at[held[b], 1], c_sem.at[b], c_rec.at[b, 1], ctx=owner).wait_send()

        @pl.when((c == owner) & (t != b))
        def _():
            remote(own_g.at[0, b], rz.at[held[b], 0], z_sem.at[b], z_rec.at[b, 0], tp=t).wait_send()
    for s in range(S):
        ag_drain(s)


def finish(dq, dkv, received, normed, wall, g, start, dmid, gain, small, pick, counts):
    F, C, T = counts
    _, S, part, own_rows = dq.shape
    width = normed.shape[2]
    _, _, shard_rows, wide = g.shape
    bf, f32 = jnp.bfloat16, jnp.float32
    rows = own_rows * T
    extra = 8 + pick.shape[1]
    mine = -(-T // C)
    vmem = pl.BlockSpec(memory_space=pltpu.VMEM)
    anywhere = pl.BlockSpec(memory_space=pl.ANY)
    dma = lambda *shape: pltpu.SemaphoreType.DMA(shape)
    return pl.pallas_call(
        functools.partial(finish_kernel, counts),
        in_specs=[vmem, vmem, vmem, anywhere, anywhere, anywhere, vmem, vmem, vmem, vmem, vmem],
        out_specs=[anywhere, vmem, vmem, vmem],
        out_shape=[
            jax.ShapeDtypeStruct((S, rows, width), bf),
            jax.ShapeDtypeStruct((shard_rows, wide), bf),
            jax.ShapeDtypeStruct((3 * part, shard_rows), f32),
            jax.ShapeDtypeStruct((extra, width), f32),
        ],
        scratch_shapes=[
            pltpu.VMEM((T, S, 2 * part, own_rows), bf),
            pltpu.VMEM((T, S, part, own_rows), bf),
            pltpu.VMEM((T, S, 2 * part, own_rows), bf),
            pltpu.VMEM((S, rows, width), bf),
            pltpu.VMEM((T, 3, width, part), bf),
            pltpu.VMEM((2, T, shard_rows, wide), bf),
            pltpu.VMEM((T, 2, shard_rows, wide), bf),
            pltpu.VMEM((T, shard_rows, wide), bf),
            pltpu.VMEM((mine, C, shard_rows, wide), bf),
            pltpu.VMEM((mine, 2, shard_rows, wide), bf),
            pltpu.VMEM((3 * part, width), f32),
            pltpu.VMEM((F, 3 * part, shard_rows), bf),
            pltpu.VMEM((F, 3 * part, shard_rows), bf),
            pltpu.VMEM((shard_rows, wide), bf),
            pltpu.VMEM((C, 3 * part, shard_rows), bf),
            pltpu.VMEM((S, own_rows, width), bf),
            pltpu.VMEM((extra, width), f32),
            pltpu.VMEM((T, extra, width), f32),
            pltpu.VMEM((C, extra, width), f32),
            pltpu.VMEM((F, extra, width), f32),
            dma(T, 2), dma(T, 2), dma(T), dma(T), dma(T), dma(T, C), dma(T), dma(T, 2), dma(C), pltpu.SemaphoreType.DMA,
            dma(T, S), dma(T, S), dma(T, S), dma(T, S), dma(S, T, 2), dma(S, T, 2), dma(F), dma(F), dma(C), dma(C),
            dma(T), dma(T), dma(C), dma(C), dma(F), dma(F), dma(2 + T * F), dma(2),
        ],
        compiler_params=pltpu.CompilerParams(
            vmem_limit_bytes=VMEM_LIMIT, collective_id=0, has_side_effects=True
        ),
        cost_estimate=pl.CostEstimate(flops=4 * 10**9, bytes_accessed=64 << 20, transcendentals=0),
    )(dq, dkv, received, normed, wall, g, start, dmid, gain, small, pick)


def local(
    inputs, thoughts, positions, lengths, w_qkv, w_out, w_fc, w_proj, norm_gains, norm_biases, out_grad,
):
    rows, seqs, width = inputs.shape
    ctx_count = lax.axis_size("ctx")
    tp_count = lax.axis_size("tp")
    fsdp_count = lax.axis_size("fsdp")
    ctx, tp, fsdp = lax.axis_index("ctx"), lax.axis_index("tp"), lax.axis_index("fsdp")
    first_row = ctx * rows
    own_rows = rows // tp_count
    own_tokens = own_rows * seqs
    far = min(ctx_count - 1, -(-(DOC_MOST - 1) // rows))
    block = min(256, rows)
    bf, f32 = jnp.bfloat16, jnp.float32

    qkv_full = lax.all_gather(w_qkv, "fsdp", axis=1, tiled=True)
    params = lax.all_gather(jnp.concatenate([norm_gains, norm_biases]), "fsdp", axis=1, tiled=True).astype(f32)
    gains, biases = params[:2], params[2:]
    everywhere = lambda w, axes: functools.reduce(
        lambda v, pair: lax.all_gather(v, pair[0], axis=pair[1], tiled=True), axes, w
    )
    out_full = everywhere(w_out, (("tp", 0), ("fsdp", 1)))
    fc_full = everywhere(w_fc, (("tp", 1), ("fsdp", 0)))
    proj_full_t = everywhere(w_proj.T, (("tp", 1), ("fsdp", 0)))
    qkv_all = lax.all_gather(w_qkv, ("tp", "fsdp"), axis=0, tiled=False)

    local_width = qkv_full.shape[2]
    qkv_matrix = jnp.transpose(qkv_full, (1, 0, 2)).reshape(width, 3 * local_width)
    places = first_row + jnp.arange(rows, dtype=jnp.int32)
    is_thought = places[None, None, :] == positions[:, :, None]
    keep = jnp.logical_not(jnp.any(is_thought, axis=0))
    start = jnp.transpose(inputs, (1, 0, 2))
    for t in range(thoughts.shape[0]):
        start = jnp.where(is_thought[t][:, :, None], thoughts[t][:, None, :], start)
    hat, inv = hat_rows(start.astype(f32))
    normed = (hat * gains[0] + biases[0]).astype(bf)
    normed_flat = normed.reshape(seqs * rows, width)
    qkv = dot(normed_flat, qkv_matrix).astype(bf).reshape(seqs, rows, 3 * local_width)

    ends = jnp.cumsum(lengths, axis=1, dtype=jnp.int32)
    low = jnp.max(jnp.where(ends[:, :, None] <= places[None, None, :], ends[:, :, None], 0), axis=1)
    low = low - (first_row - far * rows)
    first = low[:, ::block] // block

    kv = qkv[:, :, local_width:]
    prev = None
    if far:
        prev = jnp.concatenate(
            [
                lax.ppermute(kv, "ctx", [(i, i + d) for i in range(ctx_count - d)])
                for d in range(far, 0, -1)
            ],
            axis=1,
        )
    low3 = low[:, None, :]
    attended, out_t, logs = attend(qkv, prev, low3, first, block, tp_count)

    own = lambda a: lax.dynamic_slice_in_dim(a, tp * own_rows, own_rows, 1)
    exchange = lambda a: lax.all_to_all(a, "tp", split_axis=0, concat_axis=0, tiled=True)
    attended_own = exchange(attended).reshape(tp_count, own_tokens, local_width)
    start_own = own(start)
    grad_own = jnp.transpose(
        lax.dynamic_slice_in_dim(out_grad, tp * own_rows, own_rows, 0), (1, 0, 2)
    ).reshape(own_tokens, width)
    output_own, d_attended_own, d_middle, g, small = feed(
        attended_own, start_own.reshape(own_tokens, width), grad_own, out_full, params, fc_full, proj_full_t, fsdp_count
    )
    d_attended = exchange(d_attended_own.reshape(tp_count, seqs, own_rows, local_width))
    output = lax.all_gather(output_own.reshape(seqs, own_rows, width), "tp", axis=1, tiled=True)
    output = jnp.transpose(output, (1, 0, 2))

    d_q, d_kv, d_prev = attend_back(qkv, prev, low3, first, d_attended, out_t, logs, block)
    if far == 0:
        received = jnp.zeros(d_kv.shape, bf)
    else:
        pieces = [
            lax.ppermute(d_prev[index], "ctx", [(i + d, i) for i in range(ctx_count - d)])
            for index, d in enumerate(range(far, 0, -1))
        ]
        received = pieces[0] if far == 1 else sum(piece.astype(f32) for piece in pieces)

    own_places = lax.dynamic_slice_in_dim(places, tp * own_rows, own_rows, 0)
    count = thoughts.shape[0]
    pick = (own_places[None, None, :] == positions[:, :, None]).astype(bf)
    picks = []
    for s in range(seqs):
        picks.append(jnp.concatenate(
            [jnp.where(k == s, pick[:, s], jnp.zeros_like(pick[:, s])) for k in range(seqs)], axis=0
        ))
    pick = jnp.stack(picks)
    pick = jnp.pad(pick, ((0, 0), (0, -(-pick.shape[1] // 16) * 16 - pick.shape[1]), (0, 0)))
    wall = qkv_all.reshape((tp_count, fsdp_count) + w_qkv.shape)
    d_start, gw, gq, small = finish(
        d_q, d_kv, received, normed, wall, g, start_own, d_middle.reshape(seqs, own_rows, width),
        gains[0:1], small, pick, (fsdp_count, ctx_count, tp_count),
    )
    d_inputs = jnp.transpose(jnp.where(keep[:, :, None], d_start.astype(f32), 0.0), (1, 0, 2))
    d_thoughts = jnp.transpose(small[8 : 8 + count * seqs].reshape(seqs, count, width), (1, 0, 2))
    hidden = w_fc.shape[1]
    gw = gw.astype(f32)
    norms = lax.dynamic_slice_in_dim(small[:4], fsdp * w_fc.shape[0], w_fc.shape[0], 1)
    return (
        output,
        d_inputs,
        d_thoughts,
        jnp.transpose(gq.reshape(3, local_width, -1), (0, 2, 1)),
        gw[:, 2 * hidden : 2 * hidden + local_width].T,
        gw[:, :hidden],
        gw[:, hidden : 2 * hidden].T,
        norms[:2],
        norms[2],
        norms[3],
    )


def solution(mesh):
    in_specs = (
        P("ctx", "fsdp", None),
        P(None, "fsdp", None),
        P(None, "fsdp"),
        P("fsdp", None),
        P(None, "fsdp", "tp"),
        P("tp", "fsdp"),
        P("fsdp", "tp"),
        P("tp", "fsdp"),
        P(None, "fsdp"),
        P(None, "fsdp"),
        P("ctx", "fsdp", None),
    )
    out_specs = (
        P("ctx", "fsdp", None),
        P("ctx", "fsdp", None),
        P(None, "fsdp", None),
        P(None, "fsdp", "tp"),
        P("tp", "fsdp"),
        P("fsdp", "tp"),
        P("tp", "fsdp"),
        P(None, "fsdp"),
        P("fsdp"),
        P("fsdp"),
    )
    return jax.shard_map(local, mesh=mesh, in_specs=in_specs, out_specs=out_specs, check_vma=False)
```

time: 777 us -> 640 us (0.82)
  Pallas kernels: 60 us -> 300 us
  waiting for transfers between devices: 358 us -> 169 us
  blocking collectives: 105 us -> 37.1 us
  matrix products: 68 us -> 3.45 us
  local copies, waits for them, and re-layouts: 104 us -> 64.3 us
  other arithmetic: 34.1 us -> 18.6 us
    pallas_call x0 -> x2, Pallas kernels: none -> 246 us  [the longest x1 216 us: finish(): pl.pallas_call(functools.partial(finish_kernel, counts), in_specs=[vmem,...]
    all_gather x1, waiting for transfers between devices: 63.2 us -> 0.01 us  [local(): qkv_all = lax.all_gather(w_qkv, ('tp', 'fsdp'), axis=0, tiled=False)]
    dot_general x11 -> x1, matrix products: 61.3 us -> 3.45 us  [dot(): lax.dot_general(a, b, (dims, ((), ())), preferred_element_type=jnp.float32)]
    reduce_scatter x5 -> x0, waiting for transfers between devices: 44.7 us -> none  [local(): lax.psum_scatter(v, pair[0], scatter_dimension=pair[1], tiled=True)]
    all_to_all x2, waiting for transfers between devices: 94.6 us -> 55.3 us  [local(): lax.all_to_all(a, 'tp', split_axis=0, concat_axis=0, tiled=True)]
    all_gather x2 -> x1, blocking collectives: 42.2 us -> 14 us  [local(): lax.all_gather(v, pair[0], axis=pair[1], tiled=True)]
    unnamed x20 -> x7, waiting for transfers between devices: 27.6 us -> 1.96 us
    psum x2 -> x0, blocking collectives: 21.6 us -> none  [the longest x1 13.9 us: local(): lax.psum(lax.psum_scatter(small, 'fsdp', scatter_dimension=1, tiled=True)...]
  transfers between devices with their start and end apart: 21 -> 11, of which waited for: 11 -> 6; matrix products, arithmetic and copies ran while one was open for 22% -> 12% of each run, Pallas kernels for 8% -> 48%
where the time goes in v2:
time: 640 us; the launch traced here: 628 us
  Pallas kernels  300 us (47%)
  waiting for transfers between devices  169 us (26%)
  local copies, waits for them, and re-layouts  64.3 us (10%)
  blocking collectives  37.1 us (6%)
  starting transfers between devices  20.5 us (3%)
  other arithmetic  18.6 us (3%)
  between operations  14.7 us (2%)
    pallas_call x1, Pallas kernels, finish(): pl.pallas_call(functools.partial(finish_kernel, counts), in_specs=[vmem,...  216 us
    all_to_all x2, waiting for transfers between devices, local(): lax.all_to_all(a, 'tp', split_axis=0, concat_axis=0, tiled=True)  55.3 us
    all_gather x5, waiting for transfers between devices, local(): lax.all_gather(v, pair[0], axis=pair[1], tiled=True)  48.1 us
    ppermute x1, waiting for transfers between devices, local(): lax.ppermute(kv, 'ctx', [(i, i + d) for i in range(ctx_count - d)])  32.1 us
    ppermute x1, waiting for transfers between devices, local(): lax.ppermute(d_prev[index], 'ctx', [(i + d, i) for i in range(ctx_count -...  31.7 us
    pallas_call x1, Pallas kernels, feed(): pl.pallas_call(functools.partial(feed_kernel, step_cols), grid=(parts,),...  30.8 us
    pallas_call x1, Pallas kernels, attend_back(): pl.pallas_call(functools.partial(attend_back_kernel, heads, far, block),...  29.2 us
    unnamed x48, local copies, waits for them, and re-layouts  26.3 us
  transfers between devices with their start and end apart: 11, of which 6 were waited for; matrix products, arithmetic and copies ran while one was open for 12% of the time, Pallas kernels for 48%

profile of v2, /device:TPU:25, one launch (start us, length us, event | category | flops | bytes accessed | tf_op | source)
XLA Modules:
  0.0 627.6 jit_solution(2085051231550913373)
XLA Ops:
  8.7 14.0 %all_gather.35 = bf16[768,192]{1,0:T(8,128)(2,1)S(1)} all-gather(bf16[192,192]{1,0:T(8,128)(2,1)} %param.16), channel_id=1, replica_groups=mesh['fsdp'=4,'ctx'=2,'tp'=4] {'tp'}, dimensions={0}, use_global_device_ids=true | all-gather | bytes 368640 | tf_op jit(solution)/shard_map/all_gather | solution.py:841
  23.7 17.2 %all-gather.12.cloned.1.call-done = bf16[192,3072]{1,0:T(8,128)(2,1)} async-done(((bf16[192,768]{1,0:T(8,128)(2,1)}), bf16[192,3072]{1,0:T(8,128)(2,1)}) %all-gather.12.cloned.1.call-update) | async-done | bytes 1179664 | tf_op jit(solution)/shard_map/all_gather | solution.py:841
  41.0 30.8 %all-gather.16.cloned.1.call-done = bf16[192,3072]{1,0:T(8,128)(2,1)} async-done(((bf16[192,768]{1,0:T(8,128)(2,1)}), bf16[192,3072]{1,0:T(8,128)(2,1)}) %all-gather.16.cloned.1.call-update) | async-done | bytes 1179664 | tf_op jit(solution)/shard_map/all_gather | solution.py:841
  75.3 8.0 %convert_reduce_fusion = (f32[2,1024]{1,0:T(2,128)S(1)}, bf16[2,1024,768]{2,1,0:T(8,128)(2,1)S(1)}) fusion(bf16[1024,2,768]{2,1,0:T(2,128)(2,1)} %param.11, bf16[2,768]{1,0:T(2,128)(2,1)S(1)} %get-tuple-element.106, pred[2,1024]{1,0:T(4,128)(4,1)S(1)} %get-tuple-element.97, bf16[2,768]{1,0:T(2,128)(2,1)S(1)} %get-tuple-element.107, ...), kind=kLoop, calls=%fused_computation.1 | loop fusion | flops 12580864 | bytes 6330368 | tf_op jit(solution)/shard_map/reduce_sum | solution.py:21
  86.7 5.7 all-gather.1
  94.4 2.0 slice_reduce_fusion.1
  96.4 17.4 %all_gather.34 = bf16[3,768,192]{2,0,1:T(4,128)(2,1)} all-gather(bf16[3,192,192]{2,0,1:T(4,128)(2,1)S(1)} %copy.82), channel_id=1, replica_groups=mesh['fsdp'=4,'ctx'=2,'tp'=4] {'fsdp'}, dimensions={1}, use_global_device_ids=true | all-gather | bytes 1105920 | tf_op jit(solution)/shard_map/all_gather | solution.py:837
  113.7 3.4 copy.83
  117.2 2.8 fusion.5.normed_ref
  121.7 3.4 convolution_convert_fusion
  125.1 4.4 copy.84
  129.6 3.5 slice.119
  133.1 4.2 collective-permute-start
  137.9 32.1 %collective-permute-done.prev_ref = bf16[2,1024,384]{2,1,0:T(8,128)(2,1)} collective-permute-done((bf16[2,1024,384]{2,1,0:T(8,128)(2,1)}, bf16[2,1024,384]{2,1,0:T(8,128)(2,1)}, u32[]{:S(2)}, u32[]{:S(2)}) %collective-permute-start) | collective-permute-done | bytes 1572896 | tf_op jit(solution)/shard_map/ppermute | solution.py:871
  170.0 24.2 %shard_map.186 = (bf16[4,2,256,192]{3,2,1,0:T(8,128)(2,1)S(1)}, f32[2,192,1024]{2,1,0:T(8,128)S(1)}, f32[2,8,1024]{2,1,0:T(8,128)S(1)}) custom-call(s32[2,4]{1,0:T(2,128)S(1)} %and_select_fusion.first_ref, bf16[2,1024,576]{2,1,0:T(8,128)(2,1)} %bitcast.84, bf16[2,1024,384]{2,1,0:T(8,128)(2,1)} %collective-permute-done.prev_ref, s32[2,1,1024]{2,1,0:T(1,128)S(1)} %sub.37.low_ref), custom_call_target="tpu_custom_call" | custom-call | flops 8000000000 | bytes 8388608 | tf_op jit(solution)/shard_map/pallas_call | solution.py:116
  197.0 2.2 copy.85
  199.2 8.6 %all-to-all-start = ((bf16[4,2,256,192]{2,3,1,0:T(8,128)(2,1)}), bf16[4,2,256,192]{2,3,1,0:T(8,128)(2,1)}, u32[]{:S(2)}, u32[]{:S(2)}) async-start(bf16[4,2,256,192]{2,3,1,0:T(8,128)(2,1)} %copy.85), calls=%async_computation | async-start | bytes 1572864 | tf_op jit(solution)/shard_map/all_to_all | solution.py:880
  209.4 2.1 constant_dynamic-slice_fusion.1.start_ref
  211.4 2.4 copy.89.out_w_ref
  213.8 27.4 %all-to-all-done = bf16[4,2,256,192]{2,3,1,0:T(8,128)(2,1)} async-done(((bf16[4,2,256,192]{2,3,1,0:T(8,128)(2,1)}), bf16[4,2,256,192]{2,3,1,0:T(8,128)(2,1)}, u32[]{:S(2)}, u32[]{:S(2)}) %all-to-all-start) | async-done | bytes 786464 | tf_op jit(solution)/shard_map/all_to_all | solution.py:880
  241.2 2.2 copy.86
  243.4 30.8 %shard_map.187 = (bf16[512,768]{1,0:T(8,128)(2,1)}, bf16[4,512,192]{2,1,0:T(8,128)(2,1)}, f32[512,768]{1,0:T(8,128)}, bf16[4,4,192,1792]{3,2,1,0:T(8,128)(2,1)}, f32[8,768]{1,0:T(8,128)}) custom-call(bf16[4,512,192]{2,1,0:T(8,128)(2,1)} %bitcast.90, bf16[512,768]{1,0:T(8,128)(2,1)} %bitcast.87, bf16[512,768]{1,0:T(8,128)(2,1)} %bitcast.93, ...), custom_call_target="tpu_custom_call" | custom-call | flops 16999999488 | bytes 41943040 | tf_op jit(solution)/shard_map/pallas_call | solution.py:375
  274.2 2.3 copy.91
  276.5 5.8 all-to-all-start.1
  284.2 27.9 %all-to-all-done.1 = bf16[4,2,256,192]{2,3,1,0:T(8,128)(2,1)S(1)} async-done(((bf16[4,2,256,192]{2,3,1,0:T(8,128)(2,1)}), bf16[4,2,256,192]{2,3,1,0:T(8,128)(2,1)S(1)}, u32[]{:S(2)}, u32[]{:S(2)}) %all-to-all-start.1) | async-done | bytes 786464 | tf_op jit(solution)/shard_map/all_to_all | solution.py:880
  313.3 29.2 %shard_map.188 = (bf16[4,2,192,256]{3,2,1,0:T(8,128)(2,1)}, f32[4,2,384,256]{3,2,1,0:T(8,128)}, bf16[1,4,2,384,256]{4,3,2,1,0:T(8,128)(2,1)}) custom-call(s32[2,4]{1,0:T(2,128)} %copy-done.4, bf16[2,1024,576]{2,1,0:T(8,128)(2,1)} %bitcast.85, bf16[2,1024,384]{2,1,0:T(8,128)(2,1)} %collective-permute-done.prev_ref, s32[2,1,1024]{2,1,0:T(1,128)} %copy-done.3, ...), custom_call_target="tpu_custom_call" | custom-call | flops 16000000000 | bytes 16777216 | tf_op jit(solution)/shard_map/pallas_call | solution.py:225
  344.9 31.7 %collective-permute-done.1.rec_ref = bf16[4,2,384,256]{3,2,1,0:T(8,128)(2,1)S(1)} collective-permute-done((bf16[4,2,384,256]{3,2,1,0:T(8,128)(2,1)}, bf16[4,2,384,256]{3,2,1,0:T(8,128)(2,1)S(1)}, u32[]{:S(2)}, u32[]{:S(2)}) %collective-permute-start.1) | collective-permute-done | bytes 1572896 | tf_op jit(solution)/shard_map/ppermute | solution.py:898
  377.7 215.6 %shard_map.189 = (bf16[2,1024,768]{2,1,0:T(8,128)(2,1)}, bf16[192,1792]{1,0:T(8,128)(2,1)}, f32[576,192]{1,0:T(8,128)}, f32[24,768]{1,0:T(8,128)}) custom-call(bf16[4,2,192,256]{3,2,1,0:T(8,128)(2,1)} %get-tuple-element.30.dq_ref, f32[4,2,384,256]{3,2,1,0:T(8,128)} %get-tuple-element.31.dkv_ref, bf16[4,2,384,256]{3,2,1,0:T(8,128)(2,1)} %copy-done.10, ...), custom_call_target="tpu_custom_call" | custom-call | flops 4000000000 | bytes 67108864 | tf_op jit(solution)/shard_map/pallas_call | solution.py:780
  594.7 1.8 slice.123
  596.5 3.1 select_bitcast_fusion
  599.6 10.4 %copy.94 = f32[1024,2,768]{2,1,0:T(2,128)} copy(f32[1024,2,768]{2,0,1:T(8,128)} %select_bitcast_fusion) | data formatting | bytes 12582912
  614.7 5.9 copy.100
  (103 shorter events, 30.3 us)
Async XLA Ops:
  7.2 200.7 %copy-start = (bf16[1024,2,768]{2,1,0:T(2,128)(2,1)S(1)}, bf16[1024,2,768]{2,1,0:T(2,128)(2,1)}, u32[]{:S(2)}) copy-start(bf16[1024,2,768]{2,1,0:T(2,128)(2,1)} %param.21) | copy-start | bytes 9437188
  7.2 66.5 %copy-start.16 = (s32[6,2]{0,1:T(2,128)S(1)}, s32[6,2]{0,1:T(2,128)}, u32[]{:S(2)}) copy-start(s32[6,2]{0,1:T(2,128)} %param.13) | copy-start | bytes 148
  7.2 33.7 %all-gather.12.cloned.1.call-start = ((), (), s32[]{:S(2)}) async-start(), calls=%async_computation.3 | async-start | bytes 1474560 | tf_op jit(solution)/shard_map/all_gather | solution.py:841
  7.9 63.9 %all-gather.16.cloned.1.call-start = ((), (), s32[]{:S(2)}) async-start(), calls=%async_computation.5 | async-start | bytes 1474560 | tf_op jit(solution)/shard_map/all_gather | solution.py:841
  8.7 202.7 %all-gather.10.cloned.1.call-start = ((), (), s32[]{:S(2)}) async-start(), calls=%async_computation.2 | async-start | bytes 1474560 | tf_op jit(solution)/shard_map/all_gather | solution.py:841
  23.6 219.8 %all-gather.14.cloned.1.call-start = ((), (), s32[]{:S(2)}) async-start(), calls=%async_computation.4 | async-start | bytes 5898240 | tf_op jit(solution)/shard_map/all_gather | solution.py:841
  40.9 202.5 %all-gather.18.cloned.1.call-start = ((), (), s32[]{:S(2)}) async-start(), calls=%async_computation.6 | async-start | bytes 5898240 | tf_op jit(solution)/shard_map/all_gather | solution.py:841
  71.8 273.0 %all-gather.22.cloned.1.call-start = ((), (), s32[]{:S(2)}) async-start(), calls=%async_computation.8 | async-start | bytes 5013504 | tf_op jit(solution)/shard_map/all_gather | solution.py:846
  83.3 1.7 copy-start.7
  83.3 3.4 copy-start.19
  83.3 3.4 copy-start.20
  117.2 4.5 copy-start.11
  120.0 1.7 copy-start.8
  125.1 12.2 %copy-start.18 = (s32[2,3]{1,0:T(2,128)S(1)}, s32[2,3]{1,0:T(2,128)}, u32[]{:S(2)}) copy-start(s32[2,3]{1,0:T(2,128)} %param.14) | copy-start | bytes 76
  133.1 36.9 %collective-permute-start = (bf16[2,1024,384]{2,1,0:T(8,128)(2,1)}, bf16[2,1024,384]{2,1,0:T(8,128)(2,1)}, u32[]{:S(2)}, u32[]{:S(2)}) collective-permute-start(bf16[2,1024,384]{2,1,0:T(8,128)(2,1)} %slice.119), channel_id=1, source_target_pairs={{0,4},{1,5},{2,6},{3,7},{8,12},{9,13},{10,14},{11,15},{16,20},{17,... | collective-permute-start | bytes 4718600 | tf_op jit(solution)/shard_map/ppermute | solution.py:871
  137.8 56.5 %copy-start.3 = (s32[2,1,1024]{2,1,0:T(1,128)}, s32[2,1,1024]{2,1,0:T(1,128)S(1)}, u32[]{:S(2)}) copy-start(s32[2,1,1024]{2,1,0:T(1,128)S(1)} %sub.37.low_ref) | copy-start | bytes 24580
  137.9 56.4 %copy-start.4 = (s32[2,4]{1,0:T(2,128)}, s32[2,4]{1,0:T(2,128)S(1)}, u32[]{:S(2)}) copy-start(s32[2,4]{1,0:T(2,128)S(1)} %and_select_fusion.first_ref) | copy-start | bytes 100
  194.2 1.0 copy-start.2
  195.2 1.1 copy-start.5
  196.4 0.6 copy-start.6
  199.2 42.0 %all-to-all-start = ((bf16[4,2,256,192]{2,3,1,0:T(8,128)(2,1)}), bf16[4,2,256,192]{2,3,1,0:T(8,128)(2,1)}, u32[]{:S(2)}, u32[]{:S(2)}) async-start(bf16[4,2,256,192]{2,3,1,0:T(8,128)(2,1)} %copy.85), calls=%async_computation | async-start | bytes 1572864 | tf_op jit(solution)/shard_map/all_to_all | solution.py:880
  274.2 8.3 %copy-start.12 = (bf16[512,768]{1,0:T(8,128)(2,1)S(1)}, bf16[512,768]{1,0:T(8,128)(2,1)}, u32[]{:S(2)}) copy-start(bf16[512,768]{1,0:T(8,128)(2,1)} %get-tuple-element.26) | copy-start | bytes 2359300
  276.5 35.6 %all-to-all-start.1 = ((bf16[4,2,256,192]{2,3,1,0:T(8,128)(2,1)}), bf16[4,2,256,192]{2,3,1,0:T(8,128)(2,1)S(1)}, u32[]{:S(2)}, u32[]{:S(2)}) async-start(bf16[4,2,256,192]{2,3,1,0:T(8,128)(2,1)} %copy.91), calls=%async_computation.1 | async-start | bytes 1572864 | tf_op jit(solution)/shard_map/all_to_all | solution.py:880
  282.3 332.4 %all-gather.20.cloned.1.call-start = ((), (), s32[]{:S(2)}) async-start(), calls=%async_computation.7 | async-start | bytes 3932160 | tf_op jit(solution)/shard_map/all_gather | solution.py:890
  313.3 30.8 %copy-start.15 = (pred[2,1024]{1,0:T(4,128)(4,1)S(1)}, pred[2,1024]{1,0:T(4,128)(4,1)}, u32[]{:S(2)}) copy-start(pred[2,1024]{1,0:T(4,128)(4,1)} %get-tuple-element.92) | copy-start | bytes 6148
  313.3 30.8 %copy-start.17 = (s32[6,2]{0,1:T(2,128)S(1)}, s32[6,2]{0,1:T(2,128)}, u32[]{:S(2)}) copy-start(s32[6,2]{0,1:T(2,128)} %param.13) | copy-start | bytes 148
  342.5 34.0 %collective-permute-start.1 = (bf16[4,2,384,256]{3,2,1,0:T(8,128)(2,1)}, bf16[4,2,384,256]{3,2,1,0:T(8,128)(2,1)S(1)}, u32[]{:S(2)}, u32[]{:S(2)}) collective-permute-start(bf16[4,2,384,256]{3,2,1,0:T(8,128)(2,1)} %bitcast.103), channel_id=1, source_target_pairs={{4,0},{5,1},{6,2},{7,3},{12,8},{13,9},{14,10},{15,11},{20,16},{21,... | collective-permute-start | bytes 4718600 | tf_op jit(solution)/shard_map/ppermute | solution.py:898
  376.6 1.2 copy-start.10
  593.3 3.2 copy-start.14
  593.3 3.2 copy-start.9
  599.6 11.2 %copy-start.13 = (f32[576,192]{1,0:T(8,128)S(1)}, f32[576,192]{1,0:T(8,128)}, u32[]{:S(2)}) copy-start(f32[576,192]{1,0:T(8,128)} %get-tuple-element.38) | copy-start | bytes 1327108
  614.7 5.9 copy-start.1
Sparse Core Ops, SparseCore 0:
  9.6 31.2 all-gather.11
  42.5 29.3 all-gather.15
  74.0 18.8 all-gather.9
  94.3 40.9 all-gather.13
  136.6 38.4 all-gather.17
  177.2 65.0 all-gather.21
  284.6 67.4 all-gather.19

commit v3 on v2

--- a/solution.py
+++ b/solution.py
@@ -46,109 +46,376 @@
     return value.astype(jnp.float32).T.astype(jnp.bfloat16)
 
 
-def attend_kernel(heads, far, block, first_ref, qkv_ref, prev_ref, low_ref, out_ref, out_t_ref, log_ref, k_s, vt_s, qt_s):
-    s = pl.program_id(0)
-    rows = qkv_ref.shape[0]
-    parts, own_rows = out_ref.shape[0], out_ref.shape[1]
-    for h in range(heads):
-        qt_s[h] = turn(qkv_ref[:, column(h)].astype(jnp.float32) * 0.125)
-        if far:
-            k_s[h, : far * rows] = prev_ref[:, column(h)]
-            vt_s[h, :, : far * rows] = turn(prev_ref[:, column(heads + h)])
-        k_s[h, far * rows :] = qkv_ref[:, column(heads + h)]
-        vt_s[h, :, far * rows :] = turn(qkv_ref[:, column(2 * heads + h)])
-    for i in range(rows // block):
-        span = column(i, block)
-        low = low_ref[:, span]
-        top = far * rows + i * block + lax.broadcasted_iota(jnp.int32, (1, block), 1)
-        last = far * (rows // block) + i + 1
-
-        def step(kb, carry):
-            base = pl.multiple_of(kb * block, block)
-            here = pl.ds(base, block)
-            place = base + lax.broadcasted_iota(jnp.int32, (block, 1), 0)
-            allowed = (place >= low) & (place <= top)
-            after = []
-            for h in range(heads):
-                m, l, acc = carry[h]
-                scores = dot(k_s[h, here, :], qt_s[h, :, span])
-                scores = jnp.where(allowed, scores, MASKED)
-                m_new = jnp.maximum(m, jnp.max(scores, axis=0, keepdims=True))
-                p = jnp.exp(scores - m_new)
-                alpha = jnp.exp(m - m_new)
-                l = alpha * l + jnp.sum(p, axis=0, keepdims=True)
-                acc = alpha * acc + dot(vt_s[h, :, here], p.astype(jnp.bfloat16))
-                after.append((m_new, l, acc))
-            return tuple(after)
-
-        ends = lax.fori_loop(
-            first_ref[s, i],
-            last,
-            step,
-            tuple(
-                (
-                    jnp.full((1, block), MASKED, jnp.float32),
-                    jnp.zeros((1, block), jnp.float32),
-                    jnp.zeros((HEAD_DIM, block), jnp.float32),
-                )
-                for _ in range(heads)
-            ),
-        )
-        for h, (m, l, acc) in enumerate(ends):
-            out_t_ref[column(h), span] = acc / l
-            log_ref[h : h + 1, span] = m + jnp.log(l)
-    for t in range(parts):
-        out_ref[t] = turn_back(out_t_ref[:, column(t, own_rows)])
-
-
 def turn_back(value):
     return value.T.astype(jnp.bfloat16)
 
 
-def attend(qkv, prev, low, first, block, parts):
-    seqs, rows, width3 = qkv.shape
-    width = width3 // 3
-    heads = width // HEAD_DIM
-    far = 0 if prev is None else prev.shape[1] // rows
-    if prev is None:
-        prev = jnp.zeros((seqs, 16, 2 * width), qkv.dtype)
-    spec = lambda *shape: pl.BlockSpec((None,) + shape, lambda s, *_: (s, 0, 0))
+def front_kernel(
+    sizes, block,
+    start_ref, low_ref, wq_ref, wo_ref, wf_ref, wp_ref, par_ref,
+    att_ref, q_ref, kv_ref, prev_ref, out_t_ref, log_ref, normed_ref, ow_ref, fc_ref, pj_ref, params_ref,
+    start_s, normed_s, wl_s, wo_s, par_s, q_s, kv_s, prev_s, qt_s, ko_s, vto_s, kp_s, vtp_s, m_s, l_s, att_s,
+    in_sem, out_sem, w_loc, z_sem, z_rec, s_sem, s_rec, x_sem, x_rec, r_sem, r_rec,
+    kv_sem, kv_rec, at_sem, at_rec, at_loc,
+):
+    F, C, T = sizes
+    f, c, t = lax.axis_index("fsdp"), lax.axis_index("ctx"), lax.axis_index("tp")
+    S, rows, width = start_ref.shape
+    hw = q_ref.shape[2]
+    heads = hw // HEAD_DIM
+    own_rows = rows // T
+    far = prev_ref.shape[1] // rows if C > 1 else 0
+    shard = wq_ref.shape[1]
+    hidden = wf_ref.shape[1]
+    bf, f32 = jnp.bfloat16, jnp.float32
+    sib, across = f ^ 1, f ^ 2
+
+    def remote(src, dst, send, recv, **where):
+        return pltpu.make_async_remote_copy(
+            src_ref=src, dst_ref=dst, send_sem=send, recv_sem=recv, device_id=where, device_id_type=MESH
+        )
+
+    start_in = pltpu.make_async_copy(start_ref, start_s, in_sem.at[0])
+    start_in.start()
+
+    barrier = pltpu.get_barrier_semaphore()
+    peers = 0
+    for d in range(1, F):
+        pl.semaphore_signal(barrier, inc=1, device_id={"fsdp": f ^ d}, device_id_type=MESH)
+        peers += 1
+    for d in range(1, T):
+        pl.semaphore_signal(barrier, inc=1, device_id={"tp": lax.rem(t + d, T)}, device_id_type=MESH)
+        peers += 1
+    for d in range(1, C):
+        pl.semaphore_signal(barrier, inc=1, device_id={"ctx": lax.rem(c + d, C)}, device_id_type=MESH)
+        peers += 1
+    pl.semaphore_wait(barrier, peers)
+
+    pending = []
+
+    def go(copy):
+        copy.start()
+        pending.append(copy)
+        return copy
+
+    def at_shard(ff):
+        return pl.ds(pl.multiple_of(ff * shard, shard), shard)
+
+    def at_hidden(tt):
+        return pl.ds(pl.multiple_of(tt * hidden, hidden), hidden)
+
+    def block_at(a, tt, ff):
+        if a == 0:
+            return par_s.at[ff]
+        if a == 1:
+            return wl_s.at[:, at_shard(ff), :]
+        if a == 2:
+            return wo_s.at[tt, ff]
+        return (fc_ref if a == 3 else pj_ref).at[at_shard(ff), at_hidden(tt)]
+
+    sources = (par_ref, wq_ref, wo_ref, wf_ref, wp_ref)
+    slot = lambda d: lax.rem(t + T - d, T)
+
+    def spread_chip(a, d):
+        src = sources[a] if d == 0 else block_at(a, slot(d), f)
+        dst = block_at(a, slot(d), f)
+        go(remote(src, dst, x_sem.at[a, d], x_rec.at[a, d], fsdp=across))
+        go(remote(src, dst, s_sem.at[a, d], s_rec.at[a, d], fsdp=sib))
+
+    def take_z(a, d):
+        here = block_at(a, slot(d), f)
+        remote(here, here, z_sem.at[a, d], z_rec.at[a, d], tp=t).wait_recv()
+        spread_chip(a, d)
+
+    def relay(a, d):
+        here = block_at(a, slot(d), across)
+        remote(here, here, x_sem.at[a, d], x_rec.at[a, d], fsdp=f).wait_recv()
+        go(remote(here, here, r_sem.at[a, d], r_rec.at[a, d], fsdp=sib))
+
+    def take_chip(a, d):
+        for ff, rec in ((sib, s_rec), (sib ^ 2, r_rec)):
+            here = block_at(a, slot(d), ff)
+            remote(here, here, s_sem.at[a, d], rec.at[a, d], fsdp=f).wait_recv()
+
+    keeps = []
+    for a in range(5):
+        keep = pltpu.make_async_copy(sources[a], block_at(a, t, f), w_loc.at[a])
+        keep.start()
+        keeps.append(keep)
+    spread_chip(0, 0)
+    spread_chip(1, 0)
+    for a in (2, 3, 4):
+        for d in range(1, T):
+            go(remote(sources[a], block_at(a, t, f), z_sem.at[a, d], z_rec.at[a, d], tp=lax.rem(t + d, T)))
+        spread_chip(a, 0)
+
+    relay(0, 0)
+    take_chip(0, 0)
+    keeps[0].wait()
+    params = jnp.concatenate([par_s[ff] for ff in range(F)], axis=1)
+    params_ref[...] = params
+    start_in.wait()
+    per_seq = rows // block
+
+    def norm_one(index, _):
+        s = index // per_seq
+        here = pl.ds(pl.multiple_of(lax.rem(index, per_seq) * block, block), block)
+        hat, _ = hat_rows(start_s[s, here, :].astype(f32))
+        normed_s[s, here, :] = (hat * params_ref[0:1, :] + params_ref[2:3, :]).astype(bf)
+        return 0
+
+    lax.fori_loop(0, S * per_seq, norm_one, 0)
+    normed_out = pltpu.make_async_copy(normed_s, normed_ref, out_sem.at[0])
+    normed_out.start()
+
+    relay(1, 0)
+    take_chip(1, 0)
+    keeps[1].wait()
+
+    def kv_one(s, _):
+        def one(index, _):
+            here = pl.ds(pl.multiple_of(index * block, block), block)
+            rows_in = normed_s[s, here, :]
+            k = dot(rows_in, wl_s[1]).astype(bf)
+            v = dot(rows_in, wl_s[2]).astype(bf)
+            kv_s[s, here, :] = jnp.concatenate([k, v], axis=1)
+            v_t = turn(v)
+            for h in range(heads):
+                ko_s[s, h, here, :] = k[:, column(h)]
+                vto_s[s, h, :, here] = v_t[column(h)]
+            return 0
+
+        lax.fori_loop(0, per_seq, one, 0)
+        return 0
+
+    def kv_copy(s, d):
+        return remote(
+            kv_s.at[s], prev_s.at[s, pl.ds((far - d) * rows, rows), :],
+            kv_sem.at[d, s], kv_rec.at[d, s], ctx=lax.rem(c + d, C),
+        )
+
+    for s in range(S):
+        kv_one(s, 0)
+        for d in range(1, far + 1):
+            @pl.when(c + d < C)
+            def _():
+                kv_copy(s, d).start()
+
+    def q_one(index, _):
+        s = index // per_seq
+        here = pl.ds(pl.multiple_of(lax.rem(index, per_seq) * block, block), block)
+        q = dot(normed_s[s, here, :], wl_s[0]).astype(bf)
+        q_s[s, here, :] = q
+        q_t = turn(q.astype(f32) * 0.125)
+        for h in range(heads):
+            qt_s[s, h, :, here] = q_t[column(h)]
+        return 0
+
+    lax.fori_loop(0, S * per_seq, q_one, 0)
+    outs = [
+        pltpu.make_async_copy(q_s, q_ref, out_sem.at[1]),
+        pltpu.make_async_copy(kv_s, kv_ref, out_sem.at[2]),
+    ]
+    for copy in outs:
+        copy.start()
+
+    def own_part(s):
+        for i in range(per_seq):
+            span = column(i, block)
+            low = low_ref[s, :, span] - far * rows
+            top = i * block + lax.broadcasted_iota(jnp.int32, (1, block), 1)
+            first = max(0, i * block - (DOC_MOST - 1)) // block * block
+            many = (i + 1) * block - first
+            place = first + lax.broadcasted_iota(jnp.int32, (many, 1), 0)
+            allowed = (place >= low) & (place <= top)
+            for h in range(heads):
+                scores = dot(ko_s[s, h, first : first + many, :], qt_s[s, h, :, span])
+                scores = jnp.where(allowed, scores, MASKED)
+                m = jnp.max(scores, axis=0, keepdims=True)
+                p = jnp.exp(scores - m)
+                m_s[s, h : h + 1, span] = m
+                l_s[s, h : h + 1, span] = jnp.sum(p, axis=0, keepdims=True)
+                out_t_ref[s, column(h), span] = dot(vto_s[s, h, :, first : first + many], p.astype(bf))
+
+    def far_part(s):
+        for h in range(heads):
+            kp_s[h] = prev_s[s, :, column(h)]
+            vtp_s[h] = turn(prev_s[s, :, column(heads + h)])
+        for i in range(per_seq):
+            span = column(i, block)
+            low = low_ref[s, :, span]
+            first = max(0, far * rows + i * block - (DOC_MOST - 1)) // block * block
+            if first >= far * rows:
+                continue
+            many = far * rows - first
+            place = first + lax.broadcasted_iota(jnp.int32, (many, 1), 0)
+            allowed = place >= low
+            for h in range(heads):
+                scores = dot(kp_s[h, first : first + many, :], qt_s[s, h, :, span])
+                scores = jnp.where(allowed, scores, MASKED)
+                old = m_s[s, h : h + 1, span]
+                m = jnp.maximum(old, jnp.max(scores, axis=0, keepdims=True))
+                p = jnp.exp(scores - m)
+                alpha = jnp.exp(old - m)
+                m_s[s, h : h + 1, span] = m
+                l_s[s, h : h + 1, span] = alpha * l_s[s, h : h + 1, span] + jnp.sum(p, axis=0, keepdims=True)
+                out_t_ref[s, column(h), span] = alpha * out_t_ref[s, column(h), span] + dot(
+                    vtp_s[h, :, first : first + many], p.astype(bf)
+                )
+
+    def finish_part(s):
+        for h in range(heads):
+            out_t_ref[s, column(h), :] = out_t_ref[s, column(h), :] / l_s[s, h : h + 1, :]
+            log_ref[s, h : h + 1, :] = m_s[s, h : h + 1, :] + jnp.log(l_s[s, h : h + 1, :])
+        for tt in range(T):
+            att_s[tt, s] = turn_back(out_t_ref[s, :, column(tt, own_rows)])
+
+    for d in range(1, T):
+        take_z(2, d)
+
+    def own_loop(s, _):
+        own_part(s)
+        return 0
+
+    lax.fori_loop(0, S, own_loop, 0)
+    for d in range(T):
+        relay(2, d)
+    take_z(3, 1)
+
+    def wait_far(s):
+        for d in range(1, far + 1):
+            @pl.when(c >= d)
+            def _():
+                kv_copy(s, d).wait_recv()
+
+            @pl.when(c < d)
+            def _():
+                prev_s[s, (far - d) * rows : (far - d + 1) * rows, :] = jnp.zeros((rows, 2 * hw), bf)
+
+    at = [[None] * S for _ in range(T)]
+    for s in range(S):
+        if far:
+            wait_far(s)
+
+            @pl.when(c > 0)
+            def _():
+                far_part(s)
+        finish_part(s)
+        for d in range(1, T):
+            peer = lax.rem(t + d, T)
+            at[d][s] = go(
+                remote(att_s.at[peer, s], att_ref.at[t, s], at_sem.at[d, s], at_rec.at[d, s], tp=peer)
+            )
+        own_at = pltpu.make_async_copy(att_s.at[t, s], att_ref.at[t, s], at_loc.at[s])
+        own_at.start()
+        at[0][s] = own_at
+        if s == 0:
+            take_z(3, 2)
+            take_z(3, 3)
+            for d in range(T):
+                relay(3, d)
+    prev_out = pltpu.make_async_copy(prev_s, prev_ref, out_sem.at[3])
+    if far:
+        prev_out.start()
+    for d in range(1, T):
+        take_z(4, d)
+    for d in range(T):
+        take_chip(2, d)
+    keeps[2].wait()
+    for tt in range(T):
+        for ff in range(F):
+            ow_ref[column(tt, hw), column(ff, shard)] = wo_s[tt, ff]
+    for d in range(T):
+        relay(4, d)
+    for a in (3, 4):
+        for d in range(T):
+            take_chip(a, d)
+        keeps[a].wait()
+    for s in range(S):
+        at[0][s].wait()
+        for d in range(1, T):
+            at[d][s].wait_recv()
+    normed_out.wait()
+    for copy in outs:
+        copy.wait()
+    if far:
+        prev_out.wait()
+    for copy in pending:
+        copy.wait_send()
+    for s in range(S):
+        for d in range(1, far + 1):
+            @pl.when(c + d < C)
+            def _():
+                kv_copy(s, d).wait_send()
+
+
+def front(start, low, wq, wo, wf, wp, params, block, far, counts):
+    F, C, T = counts
+    S, rows, width = start.shape
+    hw = wq.shape[2]
+    shard = wq.shape[1]
+    heads = hw // HEAD_DIM
+    hidden = wf.shape[1]
+    bf, f32 = jnp.bfloat16, jnp.float32
+    vmem = pl.BlockSpec(memory_space=pltpu.VMEM)
+    anywhere = pl.BlockSpec(memory_space=pl.ANY)
+    dma = lambda *shape: pltpu.SemaphoreType.DMA(shape)
+    past = max(far, 1) * rows
+    shape = jax.ShapeDtypeStruct
     return pl.pallas_call(
-        functools.partial(attend_kernel, heads, far, block),
-        grid_spec=pltpu.PrefetchScalarGridSpec(
-            num_scalar_prefetch=1,
-            grid=(seqs,),
-            in_specs=[spec(rows, width3), spec(prev.shape[1], 2 * width), spec(1, rows)],
-            out_specs=[
-                pl.BlockSpec((parts, None, rows // parts, width), lambda s, *_: (0, s, 0, 0)),
-                spec(width, rows),
-                spec(8, rows),
-            ],
-            scratch_shapes=[
-                pltpu.VMEM((heads, (far + 1) * rows, HEAD_DIM), jnp.bfloat16),
-                pltpu.VMEM((heads, HEAD_DIM, (far + 1) * rows), jnp.bfloat16),
-                pltpu.VMEM((heads, HEAD_DIM, rows), jnp.bfloat16),
-            ],
+        functools.partial(front_kernel, counts, block),
+        in_specs=[anywhere, vmem, anywhere, anywhere, anywhere, anywhere, anywhere],
+        out_specs=[anywhere, anywhere, anywhere, anywhere, vmem, vmem, anywhere, vmem, anywhere, anywhere, vmem],
+        out_shape=[
+            shape((T, S, rows // T, hw), bf),
+            shape((S, rows, hw), bf),
+            shape((S, rows, 2 * hw), bf),
+            shape((S, past, 2 * hw), bf),
+            shape((S, hw, rows), f32),
+            shape((S, 8, rows), f32),
+            shape((S, rows, width), bf),
+            shape((T * hw, F * shard), bf),
+            shape((F * shard, T * hidden), bf),
+            shape((F * shard, T * hidden), bf),
+            shape((8, F * shard), f32),
+        ],
+        scratch_shapes=[
+            pltpu.VMEM((S, rows, width), bf),
+            pltpu.VMEM((S, rows, width), bf),
+            pltpu.VMEM((3, F * shard, hw), bf),
+            pltpu.VMEM((T, F, hw, shard), bf),
+            pltpu.VMEM((F, 8, shard), f32),
+            pltpu.VMEM((S, rows, hw), bf),
+            pltpu.VMEM((S, rows, 2 * hw), bf),
+            pltpu.VMEM((S, past, 2 * hw), bf),
+            pltpu.VMEM((S, heads, HEAD_DIM, rows), bf),
+            pltpu.VMEM((S, heads, rows, HEAD_DIM), bf),
+            pltpu.VMEM((S, heads, HEAD_DIM, rows), bf),
+            pltpu.VMEM((heads, past, HEAD_DIM), bf),
+            pltpu.VMEM((heads, HEAD_DIM, past), bf),
+            pltpu.VMEM((S, 8, rows), f32),
+            pltpu.VMEM((S, 8, rows), f32),
+            pltpu.VMEM((T, S, rows // T, hw), bf),
+            dma(1), dma(4), dma(5),
+            dma(5, T), dma(5, T), dma(5, T), dma(5, T), dma(5, T), dma(5, T), dma(5, T), dma(5, T),
+            dma(far + 1, S), dma(far + 1, S), dma(T, S), dma(T, S), dma(S),
+        ],
+        compiler_params=pltpu.CompilerParams(
+            vmem_limit_bytes=VMEM_LIMIT, collective_id=1, has_side_effects=True
         ),
-        out_shape=[
-            jax.ShapeDtypeStruct((parts, seqs, rows // parts, width), jnp.bfloat16),
-            jax.ShapeDtypeStruct((seqs, width, rows), jnp.float32),
-            jax.ShapeDtypeStruct((seqs, 8, rows), jnp.float32),
-        ],
-        compiler_params=pltpu.CompilerParams(vmem_limit_bytes=48 << 20),
-        cost_estimate=pl.CostEstimate(flops=8 * 10**9, bytes_accessed=8 << 20, transcendentals=8 << 20),
-    )(first, qkv, prev, low)
+        cost_estimate=pl.CostEstimate(flops=8 * 10**9, bytes_accessed=64 << 20, transcendentals=8 << 20),
+    )(start, low, wq, wo, wf, wp, params)
 
 
 def attend_back_kernel(
-    heads, far, block, first_ref, qkv_ref, prev_ref, low_ref, grad_ref, out_t_ref, log_ref,
+    heads, far, block, first_ref, q_ref, kv_ref, prev_ref, low_ref, grad_ref, out_t_ref, log_ref,
     dq_ref, dkv_ref, dprev_ref, k_s, kt_s, v_s, q_s, qt_s, g_s, gt_s, dqt_s, dk_s, dv_s,
 ):
     s = pl.program_id(0)
-    rows = qkv_ref.shape[0]
+    rows = q_ref.shape[0]
     parts, own_rows = grad_ref.shape[0], grad_ref.shape[1]
     for h in range(heads):
-        q = qkv_ref[:, column(h)].astype(jnp.float32) * 0.125
+        q = q_ref[:, column(h)].astype(jnp.float32) * 0.125
         q_s[h] = q.astype(jnp.bfloat16)
         qt_s[h] = turn_back(q)
         for t in range(parts):
@@ -159,10 +426,10 @@
             k_s[h, : far * rows] = k
             kt_s[h, :, : far * rows] = turn(k)
             v_s[h, : far * rows] = prev_ref[:, column(heads + h)]
-        k = qkv_ref[:, column(heads + h)]
+        k = kv_ref[:, column(h)]
         k_s[h, far * rows :] = k
         kt_s[h, :, far * rows :] = turn(k)
-        v_s[h, far * rows :] = qkv_ref[:, column(2 * heads + h)]
+        v_s[h, far * rows :] = kv_ref[:, column(heads + h)]
     dk_s[...] = jnp.zeros_like(dk_s)
     dv_s[...] = jnp.zeros_like(dv_s)
     for i in range(rows // block):
@@ -208,15 +475,11 @@
                 dkv_ref[t, column(at), :] = whole[:, column(far * parts + t, own_rows)]
 
 
-def attend_back(qkv, prev, low, first, grad, out_t, logs, block):
-    seqs, rows, width3 = qkv.shape
+def attend_back(q, kv, prev, low, first, grad, out_t, logs, block, far):
+    seqs, rows, width = q.shape
     parts = grad.shape[0]
     own_rows = rows // parts
-    width = width3 // 3
     heads = width // HEAD_DIM
-    far = 0 if prev is None else prev.shape[1] // rows
-    if prev is None:
-        prev = jnp.zeros((seqs, 16, 2 * width), qkv.dtype)
     spec = lambda *shape: pl.BlockSpec((None,) + shape, lambda s, *_: (s, 0, 0))
     chunked = lambda *shape: pl.BlockSpec((parts, None) + shape, lambda s, *_: (0, s, 0, 0))
     span = (far + 1) * rows
@@ -228,7 +491,7 @@
             num_scalar_prefetch=1,
             grid=(seqs,),
             in_specs=[
-                spec(rows, width3), spec(prev.shape[1], 2 * width), spec(1, rows),
+                spec(rows, width), spec(rows, 2 * width), spec(prev.shape[1], 2 * width), spec(1, rows),
                 chunked(own_rows, width), spec(width, rows), spec(8, rows),
             ],
             out_specs=[
@@ -255,7 +518,7 @@
         ],
         compiler_params=pltpu.CompilerParams(vmem_limit_bytes=VMEM_LIMIT),
         cost_estimate=pl.CostEstimate(flops=16 * 10**9, bytes_accessed=16 << 20, transcendentals=8 << 20),
-    )(first, qkv, prev, low, grad, out_t, logs)
+    )(first, q, kv, prev, low, grad, out_t, logs)
 
 
 def feed_kernel(
@@ -377,7 +640,7 @@
         grid=(parts,),
         in_specs=[
             whole(parts, tokens, part_cols), whole(tokens, width), whole(tokens, width), whole(width, width),
-            whole(4, width),
+            whole(8, width),
             pl.BlockSpec((width, hidden), lambda t: (0, t)),
             pl.BlockSpec((width, hidden), lambda t: (0, t)),
         ],
@@ -556,34 +819,25 @@
                 remote(own_g.at[0, b], rc.at[held[b], d], c_sem.at[b], c_rec.at[b, d], ctx=owner).wait_recv()
             add_rows(own_g.at[0, b], [rc.at[held[b], d] for d in range(1, C)])
 
-    def z_stage(b):
-        owner = b % C
-
-        def hop(step, way):
-            return remote(
-                own_g.at[0, b], rz.at[held[b], way], z_sem.at[b], z_rec.at[b, way], tp=t + step
-            )
-
-        @pl.when(c == owner)
-        def _():
-            if b < T - 1:
-                @pl.when((t >= b) & (t < T - 1))
+    def z_round(b, step):
+        def hop(to, way):
+            return remote(own_g.at[0, b], rz.at[held[b], way], z_sem.at[b], z_rec.at[b, way], tp=to)
+
+        def visit(from_end, way, before, here):
+            @pl.when((c == b % C) & here)
+            def _():
+                if step:
+                    hop(t, way).wait_recv()
+                    add_rows(own_g.at[0, b], [rz.at[held[b], way]])
+
+                @pl.when(before)
                 def _():
-                    hop(-1, 0).wait_recv()
-                    add_rows(own_g.at[0, b], [rz.at[held[b], 0]])
-
-                @pl.when(t > b)
-                def _():
-                    hop(-1, 0).start()
-            if b > 0:
-                @pl.when((t <= b) & (t > 0))
-                def _():
-                    hop(1, 1).wait_recv()
-                    add_rows(own_g.at[0, b], [rz.at[held[b], 1]])
-
-                @pl.when(t < b)
-                def _():
-                    hop(1, 1).start()
+                    hop(t - 1 if way == 0 else t + 1, way).start()
+
+        if T - 1 - step >= b and b < T - 1:
+            visit(step, 0, t > b, t == T - 1 - step)
+        if step <= b and b > 0:
+            visit(step, 1, t < b, t == step)
 
     hat, inv = [None] * S, [None] * S
     gain = gain_ref[...]
@@ -688,12 +942,14 @@
     for d in range(1, C):
         gc[d] = go(remote(rgc.at[c], rgc.at[c], gc_sem.at[d], gc_rec.at[d], ctx=lax.rem(c + d, C)))
 
-    for b in range(T):
-        ctx_wait(b)
-        z_stage(b)
-    for step in range(1, T):
-        for s in range(S):
-            ag_step(s, step)
+    for step in range(T):
+        if step:
+            for s in range(S):
+                ag_step(s, step)
+        for b in range(T):
+            if step == 0:
+                ctx_wait(b)
+            z_round(b, step)
 
     for d in range(1, T):
         st[d].wait_recv()
@@ -834,51 +1090,31 @@
     block = min(256, rows)
     bf, f32 = jnp.bfloat16, jnp.float32
 
-    qkv_full = lax.all_gather(w_qkv, "fsdp", axis=1, tiled=True)
-    params = lax.all_gather(jnp.concatenate([norm_gains, norm_biases]), "fsdp", axis=1, tiled=True).astype(f32)
-    gains, biases = params[:2], params[2:]
-    everywhere = lambda w, axes: functools.reduce(
-        lambda v, pair: lax.all_gather(v, pair[0], axis=pair[1], tiled=True), axes, w
-    )
-    out_full = everywhere(w_out, (("tp", 0), ("fsdp", 1)))
-    fc_full = everywhere(w_fc, (("tp", 1), ("fsdp", 0)))
-    proj_full_t = everywhere(w_proj.T, (("tp", 1), ("fsdp", 0)))
-    qkv_all = lax.all_gather(w_qkv, ("tp", "fsdp"), axis=0, tiled=False)
-
-    local_width = qkv_full.shape[2]
-    qkv_matrix = jnp.transpose(qkv_full, (1, 0, 2)).reshape(width, 3 * local_width)
+    counts = (fsdp_count, ctx_count, tp_count)
+    local_width = w_qkv.shape[2]
+    params = jnp.pad(jnp.concatenate([norm_gains, norm_biases]).astype(f32), ((0, 4), (0, 0)))
     places = first_row + jnp.arange(rows, dtype=jnp.int32)
     is_thought = places[None, None, :] == positions[:, :, None]
     keep = jnp.logical_not(jnp.any(is_thought, axis=0))
     start = jnp.transpose(inputs, (1, 0, 2))
     for t in range(thoughts.shape[0]):
         start = jnp.where(is_thought[t][:, :, None], thoughts[t][:, None, :], start)
-    hat, inv = hat_rows(start.astype(f32))
-    normed = (hat * gains[0] + biases[0]).astype(bf)
-    normed_flat = normed.reshape(seqs * rows, width)
-    qkv = dot(normed_flat, qkv_matrix).astype(bf).reshape(seqs, rows, 3 * local_width)
-
     ends = jnp.cumsum(lengths, axis=1, dtype=jnp.int32)
     low = jnp.max(jnp.where(ends[:, :, None] <= places[None, None, :], ends[:, :, None], 0), axis=1)
     low = low - (first_row - far * rows)
     first = low[:, ::block] // block
 
-    kv = qkv[:, :, local_width:]
-    prev = None
-    if far:
-        prev = jnp.concatenate(
-            [
-                lax.ppermute(kv, "ctx", [(i, i + d) for i in range(ctx_count - d)])
-                for d in range(far, 0, -1)
-            ],
-            axis=1,
-        )
     low3 = low[:, None, :]
-    attended, out_t, logs = attend(qkv, prev, low3, first, block, tp_count)
-
+    attended, q, kv, prev, out_t, logs, normed, out_full, fc_full, proj_full_t, params = front(
+        start, low3, w_qkv, w_out, w_fc, w_proj.T, params, block, far, counts
+    )
+    gains = params[:2]
+    w_qkv_late, attended = lax.optimization_barrier((w_qkv, attended))
+    wall = lax.all_gather(w_qkv_late, ("tp", "fsdp"), axis=0, tiled=False)
+    wall = wall.reshape((tp_count, fsdp_count) + w_qkv.shape)
     own = lambda a: lax.dynamic_slice_in_dim(a, tp * own_rows, own_rows, 1)
     exchange = lambda a: lax.all_to_all(a, "tp", split_axis=0, concat_axis=0, tiled=True)
-    attended_own = exchange(attended).reshape(tp_count, own_tokens, local_width)
+    attended_own = attended.reshape(tp_count, own_tokens, local_width)
     start_own = own(start)
     grad_own = jnp.transpose(
         lax.dynamic_slice_in_dim(out_grad, tp * own_rows, own_rows, 0), (1, 0, 2)
@@ -890,7 +1126,7 @@
     output = lax.all_gather(output_own.reshape(seqs, own_rows, width), "tp", axis=1, tiled=True)
     output = jnp.transpose(output, (1, 0, 2))
 
-    d_q, d_kv, d_prev = attend_back(qkv, prev, low3, first, d_attended, out_t, logs, block)
+    d_q, d_kv, d_prev = attend_back(q, kv, prev, low3, first, d_attended, out_t, logs, block, far)
     if far == 0:
         received = jnp.zeros(d_kv.shape, bf)
     else:
@@ -910,10 +1146,9 @@
         ))
     pick = jnp.stack(picks)
     pick = jnp.pad(pick, ((0, 0), (0, -(-pick.shape[1] // 16) * 16 - pick.shape[1]), (0, 0)))
-    wall = qkv_all.reshape((tp_count, fsdp_count) + w_qkv.shape)
     d_start, gw, gq, small = finish(
         d_q, d_kv, received, normed, wall, g, start_own, d_middle.reshape(seqs, own_rows, width),
-        gains[0:1], small, pick, (fsdp_count, ctx_count, tp_count),
+        gains[0:1], small, pick, counts,
     )
     d_inputs = jnp.transpose(jnp.where(keep[:, :, None], d_start.astype(f32), 0.0), (1, 0, 2))
     d_thoughts = jnp.transpose(small[8 : 8 + count * seqs].reshape(seqs, count, width), (1, 0, 2))

time: 640 us -> 495 us (0.77)
  waiting for transfers between devices: 169 us -> 94.2 us
  blocking collectives: 37.1 us -> 0 us
  local copies, waits for them, and re-layouts: 64.3 us -> 34 us
  Pallas kernels: 300 us -> 323 us
  starting transfers between devices: 20.5 us -> 6.27 us
    pallas_call x1, Pallas kernels: 24.2 us -> 94.4 us  [front(): pl.pallas_call(functools.partial(front_kernel, counts, block), in_specs=[...]
    pallas_call x1, Pallas kernels: 216 us -> 172 us  [finish(): pl.pallas_call(functools.partial(finish_kernel, counts), in_specs=[vmem,...]
    all_gather x3 -> x0, blocking collectives: 37.1 us -> none  [the longest x1 17.4 us: local(): qkv_full = lax.all_gather(w_qkv, 'fsdp', axis=1, tiled=True)]
    all_gather x6 -> x1, waiting for transfers between devices: 48.1 us -> 14.5 us  [local(): wall = lax.all_gather(w_qkv_late, ('tp', 'fsdp'), axis=0, tiled=False)]
    ppermute x1 -> x0, waiting for transfers between devices: 32.1 us -> none  [local(): lax.ppermute(kv, 'ctx', [(i, i + d) for i in range(ctx_count - d)])]
    all_to_all x2 -> x1, waiting for transfers between devices: 55.3 us -> 34.1 us  [local(): lax.all_to_all(a, 'tp', split_axis=0, concat_axis=0, tiled=True)]
    unnamed x48 -> x19, local copies, waits for them, and re-layouts: 26.3 us -> 15.8 us
    all_to_all x2 -> x1, starting transfers between devices: 14.4 us -> 4.7 us  [local(): lax.all_to_all(a, 'tp', split_axis=0, concat_axis=0, tiled=True)]
  transfers between devices with their start and end apart: 11 -> 4, of which waited for: 6 -> 4; matrix products, arithmetic and copies ran while one was open for 12% -> 1% of each run, Pallas kernels for 48% -> 5%
where the time goes in v3:
time: 495 us; the launch traced here: 487 us
  Pallas kernels  323 us (65%)
  waiting for transfers between devices  94.2 us (19%)
  local copies, waits for them, and re-layouts  34 us (7%)
  between operations  14.5 us (3%)
  other arithmetic  14.3 us (3%)
  starting transfers between devices  6.27 us (1%)
    pallas_call x1, Pallas kernels, finish(): pl.pallas_call(functools.partial(finish_kernel, counts), in_specs=[vmem,...  172 us
    pallas_call x1, Pallas kernels, front(): pl.pallas_call(functools.partial(front_kernel, counts, block), in_specs=[...  94.4 us
    ppermute x1, waiting for transfers between devices, local(): lax.ppermute(d_prev[index], 'ctx', [(i + d, i) for i in range(ctx_count -...  40.8 us
    all_to_all x1, waiting for transfers between devices, local(): lax.all_to_all(a, 'tp', split_axis=0, concat_axis=0, tiled=True)  34.1 us
    pallas_call x1, Pallas kernels, feed(): pl.pallas_call(functools.partial(feed_kernel, step_cols), grid=(parts,),...  30.7 us
    pallas_call x1, Pallas kernels, attend_back(): pl.pallas_call(functools.partial(attend_back_kernel, heads, far, block),...  25.8 us
    unnamed x19, local copies, waits for them, and re-layouts  15.8 us
    all_gather x1, waiting for transfers between devices, local(): wall = lax.all_gather(w_qkv_late, ('tp', 'fsdp'), axis=0, tiled=False)  14.5 us
  transfers between devices with their start and end apart: 4, of which 4 were waited for; matrix products, arithmetic and copies ran while one was open for 1% of the time, Pallas kernels for 5%

profile of v3, /device:TPU:25, one launch (start us, length us, event | category | flops | bytes accessed | tf_op | source)
XLA Modules:
  0.0 486.8 jit_solution(901222523494211942)
XLA Ops:
  7.3 0.9 copy.47
  8.3 0.8 slice_bitcast_fusion.15
  9.1 0.9 reduce_window_sum.11
  10.8 1.3 fusion.12.par_ref
  12.1 8.6 %fusion.4.start_ref = bf16[2,1024,768]{2,1,0:T(8,128)(2,1)} fusion(bf16[1024,2,768]{2,1,0:T(2,128)(2,1)} %param.11, pred[2,1024]{1,0:T(4,128)(4,1)S(1)} %get-tuple-element.103, pred[2,1024]{1,0:T(4,128)(4,1)S(1)} %get-tuple-element.104, pred[2,1024]{1,0:T(4,128)(4,1)S(1)} %get-tuple-element.105, pred[2,1024]{1,0:T(4,128)(4,1)S(1)} %get-tuple-element.106, ...), kind=kLoop, calls=%fused_computation.6 | loop fusion | flops 9437184 | bytes 6322176 | tf_op jit(solution)/shard_map/jit(_where)/select_n | solution.py:1101
  20.7 94.4 %shard_map.186 = (bf16[4,2,256,192]{3,2,1,0:T(8,128)(2,1)}, bf16[2,1024,192]{2,1,0:T(8,128)(2,1)}, bf16[2,1024,384]{2,1,0:T(8,128)(2,1)}, bf16[2,1024,384]{2,1,0...) custom-call(bf16[2,1024,768]{2,1,0:T(8,128)(2,1)} %fusion.4.start_re, ...), custom_call_target="tpu_custom_call" | custom-call | flops 8000000000 | bytes 67108864 | tf_op jit(solution)/shard_map/pallas_call | solution.py:365
  115.1 2.1 constant_dynamic-slice_fusion.1.start_ref
  117.7 1.0 copy.50
  118.7 30.7 %shard_map.187 = (bf16[512,768]{1,0:T(8,128)(2,1)}, bf16[4,512,192]{2,1,0:T(8,128)(2,1)}, f32[512,768]{1,0:T(8,128)}, bf16[4,4,192,1792]{3,2,1,0:T(8,128)(2,1)}, f32[8,768]{1,0:T(8,128)}) custom-call(bf16[4,512,192]{2,1,0:T(8,128)(2,1)} %bitcast.81, bf16[512,768]{1,0:T(8,128)(2,1)} %bitcast.68, bf16[512,768]{1,0:T(8,128)(2,1)} %bitcast.72, ...), custom_call_target="tpu_custom_call" | custom-call | flops 16999999488 | bytes 41943040 | tf_op jit(solution)/shard_map/pallas_call | solution.py:638
  149.4 2.9 copy.51
  152.4 0.7 all-gather.6.cloned.1.call-update
  153.2 1.3 copy.52
  154.4 4.7 all-to-all-start
  159.8 34.1 %all-to-all-done = bf16[4,2,256,192]{2,3,1,0:T(8,128)(2,1)S(1)} async-done(((bf16[4,2,256,192]{2,3,1,0:T(8,128)(2,1)}), bf16[4,2,256,192]{2,3,1,0:T(8,128)(2,1)S(1)}, u32[]{:S(2)}, u32[]{:S(2)}) %all-to-all-start) | async-done | bytes 786464 | tf_op jit(solution)/shard_map/all_to_all | solution.py:1116
  193.9 1.3 copy.53.grad_ref
  195.2 25.8 %shard_map.188 = (bf16[4,2,192,256]{3,2,1,0:T(8,128)(2,1)}, f32[4,2,384,256]{3,2,1,0:T(8,128)}, bf16[1,4,2,384,256]{4,3,2,1,0:T(8,128)(2,1)}) custom-call(s32[2,4]{1,0:T(2,128)} %and_select_fusion.first_ref, bf16[2,1024,192]{2,1,0:T(8,128)(2,1)} %get-tuple-element.42.q_ref, bf16[2,1024,384]{2,1,0:T(8,128)(2,1)} %get-tuple-element.43.kv_ref, ...), custom_call_target="tpu_custom_call" | custom-call | flops 16000000000 | bytes 16777216 | tf_op jit(solution)/shard_map/pallas_call | solution.py:488
  221.0 1.5 collective-permute-start
  222.5 1.3 slice.89.gain_ref
  224.7 4.2 all-gather.4.cloned.1.call-done
  228.8 40.8 %collective-permute-done.rec_ref = bf16[4,2,384,256]{3,2,1,0:T(8,128)(2,1)S(1)} collective-permute-done((bf16[4,2,384,256]{3,2,1,0:T(8,128)(2,1)}, bf16[4,2,384,256]{3,2,1,0:T(8,128)(2,1)S(1)}, u32[]{:S(2)}, u32[]{:S(2)}) %collective-permute-start) | collective-permute-done | bytes 1572896 | tf_op jit(solution)/shard_map/ppermute | solution.py:1134
  269.6 14.5 %all-gather.6.cloned.1.call-done = bf16[48,192,192]{2,1,0:T(8,128)(2,1)} async-done(((bf16[3,192,192]{2,1,0:T(8,128)(2,1)}), bf16[48,192,192]{2,1,0:T(8,128)(2,1)}) %all-gather.6.cloned.1.call-update) | async-done | bytes 3538960 | tf_op jit(solution)/shard_map/all_gather | solution.py:1113
  284.1 172.5 %shard_map.189 = (bf16[2,1024,768]{2,1,0:T(8,128)(2,1)}, bf16[192,1792]{1,0:T(8,128)(2,1)}, f32[576,192]{1,0:T(8,128)}, f32[24,768]{1,0:T(8,128)}) custom-call(bf16[4,2,192,256]{3,2,1,0:T(8,128)(2,1)} %get-tuple-element.48.dq_ref, f32[4,2,384,256]{3,2,1,0:T(8,128)} %get-tuple-element.49.dkv_ref, bf16[4,2,384,256]{3,2,1,0:T(8,128)(2,1)} %copy-done.3, ...), custom_call_target="tpu_custom_call" | custom-call | flops 4000000000 | bytes 67108864 | tf_op jit(solution)/shard_map/pallas_call | solution.py:1036
  456.6 1.3 convert_element_type.16
  457.9 0.9 slice_bitcast_fusion
  458.8 1.8 slice.109
  460.6 0.7 select_bitcast_fusion
  461.4 7.6 %copy.55 = f32[1024,2,768]{2,1,0:T(2,128)} copy(f32[1024,2,768]{2,0,1:T(8,128)S(1)} %select_bitcast_fusion) | data formatting | bytes 12582912
  468.9 0.8 copy.57
  469.7 2.1 copy.54
  472.5 0.7 constant_dynamic-slice_fusion
  473.2 0.6 fusion.14
  473.8 5.9 %copy.60 = bf16[1024,2,768]{2,1,0:T(2,128)(2,1)} copy(bf16[1024,2,768]{2,1,0:T(2,128)(2,1)} %bitcast.69) | data formatting | bytes 6291456
  (38 shorter events, 3.7 us)
Async XLA Ops:
  7.2 110.0 %copy-start = (bf16[1024,2,768]{2,1,0:T(2,128)(2,1)S(1)}, bf16[1024,2,768]{2,1,0:T(2,128)(2,1)}, u32[]{:S(2)}) copy-start(bf16[1024,2,768]{2,1,0:T(2,128)(2,1)} %param.21) | copy-start | bytes 9437188
  7.2 221.6 %all-gather.4.cloned.1.call-start = ((), (), s32[]{:S(2)}) async-start(), calls=%async_computation.1 | async-start | bytes 3932160 | tf_op jit(solution)/shard_map/all_gather | solution.py:1126
  149.4 3.7 copy-start.4
  152.4 131.7 %all-gather.6.cloned.1.call-start = ((), (), s32[]{:S(2)}) async-start(), calls=%async_computation.2 | async-start | bytes 5013504 | tf_op jit(solution)/shard_map/all_gather | solution.py:1113
  154.4 39.5 %all-to-all-start = ((bf16[4,2,256,192]{2,3,1,0:T(8,128)(2,1)}), bf16[4,2,256,192]{2,3,1,0:T(8,128)(2,1)S(1)}, u32[]{:S(2)}, u32[]{:S(2)}) async-start(bf16[4,2,256,192]{2,3,1,0:T(8,128)(2,1)} %copy.52), calls=%async_computation | async-start | bytes 1572864 | tf_op jit(solution)/shard_map/all_to_all | solution.py:1116
  195.2 28.8 %copy-start.6 = (s32[6,2]{0,1:T(2,128)S(1)}, s32[6,2]{0,1:T(2,128)}, u32[]{:S(2)}) copy-start(s32[6,2]{0,1:T(2,128)} %param.13) | copy-start | bytes 148
  221.0 48.6 %collective-permute-start = (bf16[4,2,384,256]{3,2,1,0:T(8,128)(2,1)}, bf16[4,2,384,256]{3,2,1,0:T(8,128)(2,1)S(1)}, u32[]{:S(2)}, u32[]{:S(2)}) collective-permute-start(bf16[4,2,384,256]{3,2,1,0:T(8,128)(2,1)} %bitcast.79), channel_id=1, source_target_pairs={{4,0},{5,1},{6,2},{7,3},{12,8},{13,9},{14,10},{15,11},{20,16},{21,... | collective-permute-start | bytes 4718600 | tf_op jit(solution)/shard_map/ppermute | solution.py:1134
  269.6 14.5 %copy-start.3 = (bf16[4,2,384,256]{3,2,1,0:T(8,128)(2,1)}, bf16[4,2,384,256]{3,2,1,0:T(8,128)(2,1)S(1)}, u32[]{:S(2)}) copy-start(bf16[4,2,384,256]{3,2,1,0:T(8,128)(2,1)S(1)} %collective-permute-done.rec_ref) | copy-start | bytes 4718596
  456.6 4.1 copy-start.5
  456.6 4.1 copy-start.2
  473.8 5.9 %copy-start.1 = (bf16[1024,2,768]{2,1,0:T(2,128)(2,1)S(1)}, bf16[1024,2,768]{2,1,0:T(2,128)(2,1)}, u32[]{:S(2)}) copy-start(bf16[1024,2,768]{2,1,0:T(2,128)(2,1)} %param.21) | copy-start | bytes 9437188
Sparse Core Ops, SparseCore 0:
  152.5 76.2 all-gather.3
  231.1 52.9 all-gather.5
